TPU v7x, 512 devices: a whole 4x4x16 slice. The times are simulated.
512 devices in a mesh: row: 16 (over z), col: 32 (over x, y, core).
Axes of the slice: x: 4, y: 4, z: 16, core: 2. Of those that a mesh axis runs over, the one named last changes fastest.
Arguments:
- gate_pre: bfloat16 [2048, 16384], P('row', 'col'), may hold values from -6 to 6
- up_pre: bfloat16 [2048, 16384], P('row', 'col'), may hold values from -6 to 6
- down_weight: bfloat16 [8192, 16384], P('row', 'col'), may hold values from -0.125 to 0.125
- block_mask: int32 [64, 128], P('row', 'col'), may hold values from 0 to 1, as said below
- cotangent: bfloat16 [2048, 8192], P('row', 'col'), may hold values from -6 to 6
Outputs:
- output: bfloat16 [2048, 8192], P('row', 'col')
- d_gate: bfloat16 [2048, 16384], P('row', 'col')
- d_up: bfloat16 [2048, 16384], P('row', 'col')
- d_down: bfloat16 [8192, 16384], P('row', 'col')
Inputs may be any that keep to these rules, and one draw needn't show every extreme that they name: `block_mask`: each device's tile of 4 x 4 blocks keeps between 4 and 12 blocks; in every draw some tile keeps exactly 12.
All inputs are finite; a program needn't handle non-finite values.
Results may differ from a plain program's by a relative error of at most 0.015.
Values may be sent and summed in bfloat16 or wider, within the bound.
A program may use at most 64 MiB of HBM per device.

v0:
```python
import jax
import jax.numpy as jnp
from jax import lax
from jax.sharding import PartitionSpec as P


def rounded_f32(values):
    return lax.optimization_barrier(values.astype(jnp.bfloat16)).astype(jnp.float32)


def body(gate_pre, up_pre, down_weight, block_mask, cotangent):
    tok_rows, ff_cols = gate_pre.shape
    d_rows = down_weight.shape[0]
    tile_r, tile_c = block_mask.shape
    block_size = d_rows // tile_r
    gate_wide = gate_pre.astype(jnp.float32)
    up_wide = up_pre.astype(jnp.float32)
    activated = jax.nn.silu(gate_wide)
    hidden = (activated * up_wide).astype(jnp.bfloat16)
    expand = jnp.repeat(jnp.repeat(block_mask, block_size, axis=0), block_size, axis=1)
    masked = jnp.where(expand > 0, down_weight, jnp.zeros_like(down_weight))
    cot_row = lax.all_gather(cotangent, "col", axis=1, tiled=True)
    cot_all = lax.all_to_all(cot_row, "row", split_axis=1, concat_axis=0, tiled=True)
    panel = lax.all_gather(masked, "row", axis=0, tiled=True)
    columns = lax.dot_general(
        hidden, panel, (((1,), (1,)), ((), ())), preferred_element_type=jnp.float32
    )
    y_partial = columns
    shards = panel.shape[0] // d_rows
    per_shard = jnp.einsum(
        "tnd,ndf->ntf",
        cot_row.reshape(tok_rows, shards, d_rows),
        panel.reshape(shards, d_rows, ff_cols),
        preferred_element_type=jnp.float32,
    )
    d_hidden = jnp.sum(rounded_f32(per_shard), axis=0)
    y_partial, d_hidden = (y_partial, d_hidden)
    y_summand = rounded_f32(y_partial)
    hidden_all = lax.all_gather(hidden, "row", axis=0, tiled=True)
    grad_full = lax.dot_general(
        cot_all, hidden_all, (((0,), (0,)), ((), ())), preferred_element_type=jnp.float32
    )
    output = lax.psum_scatter(
        y_summand.astype(jnp.bfloat16), "col", scatter_dimension=1, tiled=True
    )
    sigmoid_g = jax.nn.sigmoid(gate_wide)
    d_gate = (d_hidden * up_wide * sigmoid_g * (1.0 + gate_wide * (1.0 - sigmoid_g))).astype(
        jnp.bfloat16
    )
    d_up = (d_hidden * activated).astype(jnp.bfloat16)
    d_down = jnp.where(expand > 0, grad_full, jnp.zeros_like(grad_full)).astype(jnp.bfloat16)
    return (output, d_gate, d_up, d_down)


def solution(mesh):
    in_specs = (P("row", "col"), P("row", "col"), P("row", "col"), P("row", "col"), P("row", "col"))
    out_specs = (P("row", "col"), P("row", "col"), P("row", "col"), P("row", "col"))
    return jax.shard_map(body, mesh=mesh, in_specs=in_specs, out_specs=out_specs, check_vma=False)
```

profile of v0, /device:TPU:6, one launch (start us, length us, event | category | flops | bytes accessed | tf_op | source)
XLA Modules:
  0.0 470.4 jit_solution(9010206070040514916)
XLA Ops:
  7.2 0.0 copy-start
  7.2 0.0 copy-start.1
  7.2 0.0 all-gather.6.cloned.1.call-start
  7.2 1.6 copy.32
  8.9 0.0 all-gather.6.cloned.1.call-update
  8.9 0.0 all-gather.4.cloned.1.call-start
  8.9 0.7 broadcast_compare_fusion
  9.6 0.1 copy.29
  9.7 0.1 broadcast_bitcast_fusion
  9.8 1.3 copy.30
  11.1 0.8 bitcast_select_fusion.1
  11.9 0.0 all-gather.4.cloned.1.call-update
  11.9 0.0 copy-done
  12.0 0.1 copy.27
  12.1 0.0 copy-done.1
  12.1 0.1 copy.28
  12.2 62.5 %all-gather.6.cloned.1.call-done = bf16[128,8192]{0,1:T(8,128)(2,1)} async-done(((bf16[128,256]{0,1:T(8,128)(2,1)}), bf16[128,8192]{0,1:T(8,128)(2,1)}) %all-gather.6.cloned.1.call-update) | async-done | bytes 2097168 | tf_op jit(solution)/shard_map/all_gather | solution.py:22
  74.7 12.3 %all-to-all-start = ((bf16[128,16,512]{0,2,1:T(8,128)(2,1)}), bf16[128,16,512]{0,2,1:T(8,128)(2,1)S(1)}, u32[]{:S(2)}, u32[]{:S(2)}) async-start(bf16[128,16,512]{0,2,1:T(8,128)(2,1)} %bitcast.33), calls=%async_computation.1 | async-start | bytes 4194304 | tf_op jit(solution)/shard_map/all_to_all | solution.py:23
  87.0 0.0 all-gather.8.cloned.1.call-start
  87.0 179.0 %all-gather.4.cloned.1.call-done = bf16[8192,512]{0,1:T(8,128)(2,1)} async-done(((bf16[512,512]{0,1:T(8,128)(2,1)}), bf16[8192,512]{0,1:T(8,128)(2,1)}) %all-gather.4.cloned.1.call-update) | async-done | bytes 8388624 | tf_op jit(solution)/shard_map/all_gather | solution.py:24
  266.0 11.9 %copy.31 = bf16[8192,512]{1,0:T(8,128)(2,1)} copy(bf16[8192,512]{0,1:T(8,128)(2,1)} %all-gather.4.cloned.1.call-done) | data formatting | bytes 16777216 | tf_op jit(solution)/shard_map/all_gather | solution.py:24
  277.9 6.5 %convert_bitcast_fusion = bf16[16,128,512]{1,2,0:T(8,128)(2,1)S(1)} fusion(bf16[16,512,512]{2,1,0:T(8,128)(2,1)} %bitcast.30, bf16[128,16,512]{0,2,1:T(8,128)(2,1)} %bitcast.34), kind=kOutput, calls=%fused_computation.2 | convolution fusion | flops 1074790400 | bytes 12582912 | tf_op jit(solution)/shard_map/tnd,ndf->ntf/dot_general | solution.py:30
  284.4 0.3 convert_reduce_fusion
  284.7 0.8 multiply_convert_fusion
  285.5 0.0 all-gather.8.cloned.1.call-update
  285.5 0.0 reduce-scatter.2.cloned.1.call-start
  285.6 6.1 %convolution_convert_fusion = bf16[128,8192]{1,0:T(8,128)(2,1)} fusion(bf16[128,512]{0,1:T(8,128)(2,1)} %get-tuple-element.22, bf16[8192,512]{0,1:T(8,128)(2,1)} %all-gather.4.cloned.1.call-done), kind=kOutput, calls=%fused_computation | convolution fusion | flops 1074790400 | bytes 10616832 | tf_op jit(solution)/shard_map/dot_general | solution.py:25
  291.7 0.0 reduce-scatter.2.cloned.1.call-update
  291.7 0.0 all-to-all-done
  291.8 2.6 copy.35
  294.4 0.8 copy.36
  295.1 0.8 copy.37
  295.9 65.9 %all-gather.8.cloned.1.call-done = bf16[2048,512]{0,1:T(8,128)(2,1)} async-done(((bf16[128,512]{0,1:T(8,128)(2,1)}), bf16[2048,512]{0,1:T(8,128)(2,1)}) %all-gather.8.cloned.1.call-update) | async-done | bytes 2097168 | tf_op jit(solution)/shard_map/all_gather | solution.py:39
  361.8 3.5 fusion
  365.3 1.0 copy.38
  366.3 97.5 %reduce-scatter.2.cloned.1.call-done = bf16[128,256]{1,0:T(8,128)(2,1)} async-done(((bf16[128,8192]{1,0:T(8,128)(2,1)}), bf16[128,256]{1,0:T(8,128)(2,1)}) %reduce-scatter.2.cloned.1.call-update) | async-done | bytes 65552 | tf_op jit(solution)/shard_map/reduce_scatter | solution.py:43
  (1 shorter events, 0.0 us)
Async XLA Ops:
  7.2 4.8 %copy-start = (bf16[128,512]{1,0:T(8,128)(2,1)S(1)}, bf16[128,512]{1,0:T(8,128)(2,1)}, u32[]{:S(2)}) copy-start(bf16[128,512]{1,0:T(8,128)(2,1)} %param.5) | copy-start | bytes 393220
  7.2 4.9 %copy-start.1 = (bf16[128,512]{1,0:T(8,128)(2,1)S(1)}, bf16[128,512]{1,0:T(8,128)(2,1)}, u32[]{:S(2)}) copy-start(bf16[128,512]{1,0:T(8,128)(2,1)} %param.6) | copy-start | bytes 393220
  7.2 67.5 %all-gather.6.cloned.1.call-start = ((), (), s32[]{:S(2)}) async-start(), calls=%async_computation.4 | async-start | bytes 2162688 | tf_op jit(solution)/shard_map/all_gather | solution.py:22
  8.9 257.1 %all-gather.4.cloned.1.call-start = ((), (), s32[]{:S(2)}) async-start(), calls=%async_computation.2 | async-start | bytes 8912896 | tf_op jit(solution)/shard_map/all_gather | solution.py:24
  74.7 217.1 %all-to-all-start = ((bf16[128,16,512]{0,2,1:T(8,128)(2,1)}), bf16[128,16,512]{0,2,1:T(8,128)(2,1)S(1)}, u32[]{:S(2)}, u32[]{:S(2)}) async-start(bf16[128,16,512]{0,2,1:T(8,128)(2,1)} %bitcast.33), calls=%async_computation.1 | async-start | bytes 4194304 | tf_op jit(solution)/shard_map/all_to_all | solution.py:23
  87.0 274.9 %all-gather.8.cloned.1.call-start = ((), (), s32[]{:S(2)}) async-start(), calls=%async_computation.5 | async-start | bytes 2228224 | tf_op jit(solution)/shard_map/all_gather | solution.py:39
  285.5 178.3 %reduce-scatter.2.cloned.1.call-start = ((), (), s32[]{:S(2)}) async-start(), calls=%async_computation.3 | async-start | bytes 2162688 | tf_op jit(solution)/shard_map/reduce_scatter | solution.py:43
Sparse Core Ops, SparseCore 0:
  11.7 62.9 all-gather.5
  77.3 188.6 all-gather.3
  285.6 76.1 all-gather.7
  366.7 97.1 reduce-scatter.1
where the time goes:
time: 471 us; the launch traced here: 470 us
  waiting for transfers between devices  405 us (86%)
  local copies, waits for them, and re-layouts  20.3 us (4%)
  matrix products  16.1 us (3%)
  between operations  13.8 us (3%)
  starting transfers between devices  12.4 us (3%)
    all_gather x1, waiting for transfers between devices, body(): panel = lax.all_gather(masked, 'row', axis=0, tiled=True)  179 us
    reduce_scatter x1, waiting for transfers between devices, body(): lax.psum_scatter(y_summand.astype(jnp.bfloat16), 'col', scatter_dimension...  97.5 us
    all_gather x1, waiting for transfers between devices, body(): hidden_all = lax.all_gather(hidden, 'row', axis=0, tiled=True)  65.9 us
    all_gather x1, waiting for transfers between devices, body(): cot_row = lax.all_gather(cotangent, 'col', axis=1, tiled=True)  62.5 us
    all_to_all x1, starting transfers between devices, body(): lax.all_to_all(cot_row, 'row', split_axis=1, concat_axis=0, tiled=True)  12.3 us
    all_gather x1, local copies, waits for them, and re-layouts, body(): panel = lax.all_gather(masked, 'row', axis=0, tiled=True)  11.9 us
  transfers between devices with their start and end apart: 5, of which 4 were waited for; matrix products, arithmetic and copies ran while one was open for 8% of the time, Pallas kernels for 0%

commit v1 on v0

v1 whole, which is shorter than its diff:
```python
import functools

import jax
import jax.numpy as jnp
from jax import lax
from jax.experimental import pallas as pl
from jax.experimental.pallas import tpu as pltpu
from jax.sharding import PartitionSpec as P

MESH = pl.DeviceIdType.MESH
SUB = 4
GRP = 4
TR = 16
TC = 128
F32 = jnp.float32
BF16 = jnp.bfloat16


def nt_dot(a, b):
    return lax.dot_general(a, b, (((1,), (1,)), ((), ())), preferred_element_type=F32)


def tn_dot(a, b):
    return lax.dot_general(a, b, (((0,), (0,)), ((), ())), preferred_element_type=F32)


def kernel(nz, nq, gate_hbm, up_hbm, w_hbm, mask_ref, cot_hbm,
           out_ref, dgate_ref, dup_ref, ddown_ref,
           gate_v, up_v, wm, cot_v, hall, call, cA, cB,
           yown, ysend, yprt, ysum, yrecv, osum, oB, out_v,
           rbuf, sbuf, pbuf, acc,
           ld, ag_s, ag_r, rs_s, rs_r, cA_s, cA_r, cB_s, cB_r,
           cg_s, cg_r, rel_s, rel_r, yp_s, yp_r, yr_s, yr_r,
           oB_s, oB_r, ov_s, ov_r):
    z = lax.axis_index("row")
    col = lax.axis_index("col")
    p = lax.div(col, 2)
    c = lax.rem(col, 2)
    half = nz // 2
    tok, ffc = gate_v.shape
    dh_w = wm.shape[0] // 2
    rsub = tok // SUB
    per = nz // GRP

    def zmod(v):
        return lax.rem(v + 2 * nz, nz)

    def qmod(v):
        return lax.rem(v + 2 * nq, nq)

    def tile_rows(q):
        return pl.ds(pl.multiple_of(lax.div(q, 2) * TR, TR), TR)

    def tile_cols(q, base=0):
        return pl.ds(pl.multiple_of(base + lax.rem(q, 2) * TC, TC), TC)

    def zdev(r):
        return (r, col)

    def qdev(q):
        return (z, q * 2 + c)

    pdev = (z, p * 2 + (1 - c))
    mine = pl.multiple_of(c * dh_w, TC)
    other = pl.multiple_of((1 - c) * dh_w, TC)

    def remote(src, dst, ss, rs, dev):
        return pltpu.make_async_remote_copy(
            src_ref=src, dst_ref=dst, send_sem=ss, recv_sem=rs,
            device_id=dev, device_id_type=MESH)

    def drain(ref, sem):
        pltpu.make_async_copy(ref, ref, sem).wait()

    bar = pltpu.get_barrier_semaphore()

    @pl.loop(1, nz)
    def _(k):
        pl.semaphore_signal(bar, inc=1, device_id=zdev(zmod(z + k)), device_id_type=MESH)

    @pl.loop(1, nq)
    def _(k):
        pl.semaphore_signal(bar, inc=1, device_id=qdev(qmod(p + k)), device_id_type=MESH)

    pl.semaphore_signal(bar, inc=1, device_id=pdev, device_id_type=MESH)

    loads = [pltpu.make_async_copy(a, b, ld.at[i]) for i, (a, b) in enumerate(
        ((gate_hbm, gate_v), (up_hbm, up_v), (cot_hbm, cot_v), (w_hbm, wm)))]
    for l in loads:
        l.start()
    loads[0].wait()
    loads[1].wait()
    g = gate_v[...].astype(F32)
    hall[z] = (g / (1.0 + jnp.exp(-g)) * up_v[...].astype(F32)).astype(BF16)
    loads[2].wait()
    loads[3].wait()
    br, bc = mask_ref.shape
    bs = wm.shape[0] // br
    for i in range(br):
        for j in range(bc):
            sl = (pl.ds(i * bs, bs), pl.ds(j * bs, bs))
            keep = jnp.full((bs, bs), mask_ref[i, j], jnp.int32) > 0
            wm[sl] = jnp.where(keep, wm[sl], jnp.zeros((bs, bs), BF16))
    pl.semaphore_wait(bar, nz + nq - 1)

    def steps_of(d, u):
        return half if (u < SUB // 2) == (d == 0) else half - 1

    pairs = [(d, u, 1 - 2 * d, steps_of(d, u)) for u in range(SUB) for d in range(2)]

    def ag(d, u, sg, s):
        ref = hall.at[zmod(z - sg * s), pl.ds(u * rsub, rsub)]
        return remote(ref, ref, ag_s.at[d, u, s], ag_r.at[d, u, s], zdev(zmod(z + sg)))

    def ag_wait(d, u, sg, s):
        ref = hall.at[zmod(z - sg * (s + 1)), pl.ds(u * rsub, rsub)]
        drain(ref, ag_r.at[d, u, s])

    def y_chunk(i, slot):
        h = hall[slot]
        ysend[i] = nt_dot(h, wm[pl.ds(other, dh_w), :]).astype(BF16)
        yown[i] = nt_dot(h, wm[pl.ds(mine, dh_w), :])
        remote(ysend.at[i], yprt.at[i], yp_s, yp_r.at[i], pdev).start()

    def y_pair(i):
        drain(yprt.at[i], yp_r.at[i])
        ysum[i] = (yown[i] + yprt[i].astype(F32)).astype(BF16)

    def y_scatter(n):
        rows = pl.ds(n * per, per)
        pltpu.make_async_copy(
            ysum.at[rows, tile_rows(p), tile_cols(p)], yrecv.at[p, rows], yr_r.at[n]).start()

        @pl.loop(1, nq)
        def _(k):
            q = qmod(p + k)
            remote(ysum.at[rows, tile_rows(q), tile_cols(q)], yrecv.at[p, rows],
                   yr_s.at[n], yr_r.at[n], qdev(q)).start()

    def y_finish(n):
        rows = pl.ds(n * per, per)
        drain(yrecv.at[:, rows], yr_r.at[n])
        osum[rows] = jnp.sum(yrecv[:, rows].astype(F32), axis=0).astype(BF16)
        for i in range(n * per, (n + 1) * per):
            off = -((i + 1) // 2) if i % 2 else i // 2
            if i == 0:
                pltpu.make_async_copy(osum.at[i], oB.at[z], oB_r).start()
            else:
                remote(osum.at[i], oB.at[z], oB_s, oB_r, zdev(zmod(z + off))).start()

    for d, u, sg, n in pairs:
        ag(d, u, sg, 0).start()

    pltpu.make_async_copy(cot_v.at[tile_rows(p), tile_cols(p)], cA.at[p], cA_r).start()

    @pl.loop(1, nq)
    def _(k):
        q = qmod(p + k)
        remote(cot_v.at[tile_rows(q), tile_cols(q)], cA.at[p], cA_s, cA_r, qdev(q)).start()

    y_chunk(0, z)

    def cot_two():
        drain(cA, cA_r)
        pltpu.make_async_copy(cA.at[z], cB.at[z], cB_r).start()

        @pl.loop(1, nz)
        def _(k):
            r = zmod(z + k)
            remote(cA.at[r], cB.at[z], cB_s, cB_r, zdev(r)).start()

    def cot_region(q):
        return call.at[:, tile_rows(q), tile_cols(q, mine)]

    def cot_three():
        drain(cB, cB_r)
        pltpu.make_async_copy(cB, cot_region(p), cg_r.at[0]).start()

        @pl.loop(1, nq)
        def _(k):
            remote(cB, cot_region(p), cg_s, cg_r.at[k], qdev(qmod(p + k))).start()

    @pl.loop(1, half)
    def _(s):
        for d, u, sg, n in pairs:
            ag_wait(d, u, sg, s - 1)
            if n == half:
                ag(d, u, sg, s).start()
            else:
                @pl.when(s < n)
                def _():
                    ag(d, u, sg, s).start()
        y_chunk(2 * s - 1, zmod(z - s))
        y_chunk(2 * s, zmod(z + s))
        y_pair(2 * s - 2)

        @pl.when(s > 1)
        def _():
            y_pair(2 * s - 3)

        @pl.when(s == 1)
        def _():
            cot_two()

        @pl.when(s == half // 2)
        def _():
            y_scatter(0)
            cot_three()

    for d, u, sg, n in pairs:
        if n == half:
            ag_wait(d, u, sg, half - 1)
    y_chunk(nz - 1, zmod(z + half))

    @pl.loop(0, nq)
    def _(k):
        ref = cot_region(qmod(p - k))
        drain(ref, cg_r.at[k])
        remote(ref, ref, rel_s, rel_r, pdev).start()

    drain(call.at[:, :, pl.ds(other, dh_w)], rel_r)

    def rs(d, u, sg, s):
        rows = pl.ds(u * rsub, rsub)
        return remote(sbuf.at[d, s, rows], rbuf.at[d, s, rows],
                      rs_s.at[d, u, s], rs_r.at[d, u, s], zdev(zmod(z + sg)))

    def part(d, s):
        t = zmod(z + (1 - 2 * d) * (half - s))
        pbuf[d] = jnp.dot(call[t], wm[...], preferred_element_type=F32)

    part(0, 0)
    for d, u, sg, n in pairs:
        if n == half:
            rows = pl.ds(u * rsub, rsub)
            sbuf[d, 0, rows] = pbuf[0, rows].astype(BF16)
    for d, u, sg, n in pairs:
        if n == half:
            rs(d, u, sg, 0).start()
    part(0, 1)
    part(1, 1)
    for i in (nz - 3, nz - 2, nz - 1):
        y_pair(i)
    for n in range(1, GRP):
        y_scatter(n)

    dw_events = {1: 0, 2: 1, 3: 2, 4: 3} if half > 4 else {1: 0}
    tgrp = nz // 4

    def dw(n):
        a = call[n * tgrp:(n + 1) * tgrp].reshape(tgrp * tok, wm.shape[0])
        b = hall[n * tgrp:(n + 1) * tgrp].reshape(tgrp * tok, ffc)
        v = tn_dot(a, b)
        if n == 0:
            acc[...] = v
        else:
            acc[...] += v

    def out_two():
        drain(oB, oB_r)
        pltpu.make_async_copy(oB.at[p], out_v.at[tile_rows(p), tile_cols(p)], ov_r).start()

        @pl.loop(1, nq)
        def _(k):
            q = qmod(p + k)
            remote(oB.at[q], out_v.at[tile_rows(p), tile_cols(p)], ov_s, ov_r, qdev(q)).start()

    @pl.loop(1, half)
    def _(s):
        for d, u, sg, n in pairs:
            rows = pl.ds(u * rsub, rsub)
            if n == half:
                drain(rbuf.at[d, s - 1, rows], rs_r.at[d, u, s - 1])
                sbuf[d, s, rows] = (pbuf[d, rows] + rbuf[d, s - 1, rows].astype(F32)).astype(BF16)
            else:
                @pl.when(s > 1)
                def _():
                    drain(rbuf.at[d, s - 1, rows], rs_r.at[d, u, s - 1])
                    sbuf[d, s, rows] = (pbuf[d, rows] + rbuf[d, s - 1, rows].astype(F32)).astype(BF16)

                @pl.when(s == 1)
                def _():
                    sbuf[d, s, rows] = pbuf[d, rows].astype(BF16)
            rs(d, u, sg, s).start()

        part(0, s + 1)

        @pl.when(s < half - 1)
        def _():
            part(1, s + 1)

        if half > 4:
            for at, n in {1: 0, 2: 1, 3: 2, 4: 3}.items():
                @pl.when(s == at)
                def _():
                    dw(n)
            for at, n in {3: 0, 4: 1, 5: 2, 6: 3}.items():
                @pl.when(s == at)
                def _():
                    y_finish(n)
        else:
            for n in range(4):
                dw(n)
                y_finish(n)

    out_two()
    for d, u, sg, n in pairs:
        drain(rbuf.at[d, half - 1, pl.ds(u * rsub, rsub)], rs_r.at[d, u, half - 1])
    for n in range(SUB):
        rows = pl.ds(n * rsub, rsub)
        dh = pbuf[0, rows] + rbuf[0, half - 1, rows].astype(F32) + rbuf[1, half - 1, rows].astype(F32)
        g = gate_v[rows, :].astype(F32)
        sig = 1.0 / (1.0 + jnp.exp(-g))
        dgate_ref[rows, :] = (dh * up_v[rows, :].astype(F32) * sig * (1.0 + g * (1.0 - sig))).astype(BF16)
        dup_ref[rows, :] = (dh * (g * sig)).astype(BF16)
    for i in range(br):
        for j in range(bc):
            sl = (pl.ds(i * bs, bs), pl.ds(j * bs, bs))
            keep = jnp.full((bs, bs), mask_ref[i, j], jnp.int32) > 0
            ddown_ref[sl] = jnp.where(keep, acc[sl], jnp.zeros((bs, bs), F32)).astype(BF16)

    for d, u, sg, n in pairs:
        @pl.loop(0, n)
        def _(s):
            drain(hall.at[0, pl.ds(0, rsub)], ag_s.at[d, u, s])

        @pl.loop(half - n, half)
        def _(s):
            drain(sbuf.at[d, s, pl.ds(u * rsub, rsub)], rs_s.at[d, u, s])
    rest = pl.ds(0, nq - 1)
    drain(cA.at[rest], cA_s)
    drain(cB.at[rest], cB_s)
    drain(call.at[rest, :, pl.ds(0, dh_w)], cg_s)
    drain(call.at[:, :, pl.ds(0, dh_w)], rel_s)
    drain(ysend, yp_s)
    for n in range(GRP):
        drain(yrecv.at[rest, pl.ds(n * per, per)], yr_s.at[n])
    drain(oB.at[rest], oB_s)
    drain(oB.at[rest], ov_s)
    drain(out_v, ov_r)
    out_ref[...] = out_v[...]


def body(nz, nq, gate_pre, up_pre, down_weight, block_mask, cotangent):
    tok, ffc = gate_pre.shape
    dr = down_weight.shape[0]
    dh_w = dr // 2
    half = nz // 2
    dma = pltpu.SemaphoreType.DMA
    vm = pltpu.VMEM
    any_ = pl.BlockSpec(memory_space=pl.ANY)
    vout = pl.BlockSpec(memory_space=pltpu.VMEM)
    return pl.pallas_call(
        functools.partial(kernel, nz, nq),
        out_shape=(
            jax.ShapeDtypeStruct((tok, dh_w), BF16),
            jax.ShapeDtypeStruct((tok, ffc), BF16),
            jax.ShapeDtypeStruct((tok, ffc), BF16),
            jax.ShapeDtypeStruct((dr, ffc), BF16),
        ),
        in_specs=[any_, any_, any_, pl.BlockSpec(memory_space=pltpu.SMEM), any_],
        out_specs=(vout,) * 4,
        scratch_shapes=[
            vm((tok, ffc), BF16), vm((tok, ffc), BF16), vm((dr, ffc), BF16), vm((tok, dh_w), BF16),
            vm((nz, tok, ffc), BF16), vm((nz, tok, dr), BF16),
            vm((nq, TR, TC), BF16), vm((nz, TR, TC), BF16),
            vm((nz, tok, dh_w), F32), vm((nz, tok, dh_w), BF16), vm((nz, tok, dh_w), BF16),
            vm((nz, tok, dh_w), BF16), vm((nq, nz, TR, TC), BF16),
            vm((nz, TR, TC), BF16), vm((nz, TR, TC), BF16), vm((tok, dh_w), BF16),
            vm((2, half, tok, ffc), BF16), vm((2, half, tok, ffc), BF16),
            vm((2, tok, ffc), F32), vm((dr, ffc), F32),
            dma((4,)), dma((2, SUB, half)), dma((2, SUB, half)), dma((2, SUB, half)), dma((2, SUB, half)),
            dma, dma, dma, dma,
            dma, dma((nq,)), dma, dma, dma, dma((nz,)), dma((GRP,)), dma((GRP,)),
            dma, dma, dma, dma,
        ],
        compiler_params=pltpu.CompilerParams(
            collective_id=0, has_side_effects=True, vmem_limit_bytes=60 * 1024 * 1024),
    )(gate_pre, up_pre, down_weight, block_mask, cotangent)


def solution(mesh):
    nz = mesh.shape["row"]
    nq = mesh.shape["col"] // 2
    spec = P("row", "col")
    return jax.shard_map(functools.partial(body, nz, nq), mesh=mesh, in_specs=(spec,) * 5,
                         out_specs=(spec,) * 4, check_vma=False)
```

time: 471 us -> 98.1 us (0.21)
  waiting for transfers between devices: 405 us -> 0 us
  Pallas kernels: 0 us -> 90.7 us
  matrix products: 16.1 us -> 0 us
  local copies, waits for them, and re-layouts: 20.3 us -> 5.46 us
  between operations: 13.8 us -> 0.65 us
  starting transfers between devices: 12.4 us -> 0 us
    all_gather x3 -> x0, waiting for transfers between devices: 307 us -> none  [the longest x1 179 us: body(): panel = lax.all_gather(masked, 'row', axis=0, tiled=True)]
    reduce_scatter x1 -> x0, waiting for transfers between devices: 97.5 us -> none  [body(): lax.psum_scatter(y_summand.astype(jnp.bfloat16), 'col', scatter_dimension...]
    pallas_call x0 -> x1, Pallas kernels: none -> 90.7 us  [body(): pl.pallas_call(functools.partial(kernel, nz, nq), out_shape=(jax.ShapeDty...]
    dot_general x3 -> x0, matrix products: 16.1 us -> none  [the longest x1 6.49 us: body(): jnp.einsum('tnd,ndf->ntf', cot_row.reshape(tok_rows, shards, d_rows), pan...]
    all_to_all x1 -> x0, starting transfers between devices: 12.3 us -> none  [body(): lax.all_to_all(cot_row, 'row', split_axis=1, concat_axis=0, tiled=True)]
    all_gather x1 -> x0, local copies, waits for them, and re-layouts: 11.9 us -> none  [body(): panel = lax.all_gather(masked, 'row', axis=0, tiled=True)]
  transfers between devices with their start and end apart: 5 -> 0, of which waited for: 4 -> 0; matrix products, arithmetic and copies ran while one was open for 8% -> 0% of each run, Pallas kernels for 0% -> 0%
where the time goes in v1:
time: 98.1 us; the launch traced here: 96.8 us
  Pallas kernels  90.7 us (92%)
  local copies, waits for them, and re-layouts  5.46 us (6%)
    pallas_call x1, Pallas kernels, body(): pl.pallas_call(functools.partial(kernel, nz, nq), out_shape=(jax.ShapeDty...  90.7 us
    unnamed x6, local copies, waits for them, and re-layouts  5.46 us

profile of v1, /device:TPU:6, one launch (start us, length us, event | category | flops | bytes accessed | tf_op | source)
XLA Modules:
  0.0 96.8 jit_solution(7601313883998997005)
XLA Ops:
  0.6 90.7 %shard_map.84 = (bf16[128,256]{1,0:T(8,128)(2,1)}, bf16[128,512]{1,0:T(8,128)(2,1)}, bf16[128,512]{1,0:T(8,128)(2,1)}, bf16[512,512]{1,0:T(8,128)(2,1)}) custom-call(bf16[128,512]{1,0:T(8,128)(2,1)} %gate_hbm.1, bf16[128,512]{1,0:T(8,128)(2,1)} %up_hbm.1, bf16[512,512]{1,0:T(8,128)(2,1)} %w_hbm.1, s32[4,4]{1,0:T(4,128)} %mask_ref.1, bf16[128,256]{1,0:T(8,128)(2,1)} %cot_hbm.1), custom_call_target="tpu_custom_call" | custom-call | tf_op jit(solution)/shard_map/pallas_call | solution.py:353
  91.4 0.0 copy-start
  91.4 1.5 %copy.13 = bf16[128,256]{1,0:T(8,128)(2,1)} copy(bf16[128,256]{1,0:T(8,128)(2,1)} %get-tuple-element.8) | data formatting | bytes 131072
  92.9 1.6 %copy.14 = bf16[128,512]{1,0:T(8,128)(2,1)} copy(bf16[128,512]{1,0:T(8,128)(2,1)} %get-tuple-element.9) | data formatting | bytes 262144
  94.5 1.6 %copy.15 = bf16[128,512]{1,0:T(8,128)(2,1)} copy(bf16[128,512]{1,0:T(8,128)(2,1)} %get-tuple-element.10) | data formatting | bytes 262144
  96.0 0.0 copy-done
  96.0 0.8 copy.16
Async XLA Ops:
  91.4 4.7 %copy-start = (bf16[512,512]{1,0:T(8,128)(2,1)S(1)}, bf16[512,512]{1,0:T(8,128)(2,1)}, u32[]{:S(2)}) copy-start(bf16[512,512]{1,0:T(8,128)(2,1)} %get-tuple-element.11) | copy-start | bytes 1572868

commit v2 on v0

v2 whole, which is shorter than its diff:
```python
import functools

import jax
import jax.numpy as jnp
from jax import lax
from jax.experimental import pallas as pl
from jax.experimental.pallas import tpu as pltpu
from jax.sharding import PartitionSpec as P

MESH = pl.DeviceIdType.MESH
SUB = 4
TR = 16
TC = 128
F32 = jnp.float32
BF16 = jnp.bfloat16


def nt_dot(a, b):
    return lax.dot_general(a, b, (((1,), (1,)), ((), ())), preferred_element_type=F32)


def tn_dot(a, b):
    return lax.dot_general(a, b, (((0,), (0,)), ((), ())), preferred_element_type=F32)


def groups(nz):
    half = nz // 2
    if half <= 4:
        return [(i, i + 1) for i in range(nz)]
    cut = [0, 5, 9, 13, nz]
    return list(zip(cut[:-1], cut[1:]))


def kernel(nz, nq, gate_hbm, up_hbm, w_hbm, mask_ref, cot_hbm,
           out_hbm, dh_hbm, dw_hbm,
           gate_v, up_v, wm, cot_v, hall, call, cA, cB,
           yown, ysend, yprt, ysum, yrecv, osum, oB, out_v,
           rbuf, sbuf, pbuf, acc, accb,
           ld, ag_s, ag_r, rs_s, rs_r, cA_s, cA_r, cB_s, cB_r,
           cg_s, cg_r, rel_s, rel_r, yp_s, yp_r, yr_s, yr_r,
           oB_s, oB_r, ov_s, ov_r, st):
    z = lax.axis_index("row")
    col = lax.axis_index("col")
    p = lax.div(col, 2)
    c = lax.rem(col, 2)
    half = nz // 2
    tok, ffc = gate_v.shape
    dr = wm.shape[0]
    dw_h = dr // 2
    rsub = tok // SUB
    big = half > 4
    grps = groups(nz)

    def zdev(k):
        return (lax.rem(z + (k + nz), nz), col)

    def qmod(v):
        return lax.rem(v + nq, nq)

    def tile(q):
        return (pl.ds(pl.multiple_of(lax.div(q, 2) * TR, TR), TR),
                pl.ds(pl.multiple_of(lax.rem(q, 2) * TC, TC), TC))

    def qdev(q):
        return (z, q * 2 + c)

    pdev = (z, p * 2 + (1 - c))
    mine = pl.multiple_of(c * dw_h, TC)
    other = pl.multiple_of((1 - c) * dw_h, TC)

    def remote(src, dst, ss, rs, dev):
        return pltpu.make_async_remote_copy(
            src_ref=src, dst_ref=dst, send_sem=ss, recv_sem=rs,
            device_id=dev, device_id_type=MESH)

    def local(src, dst, sem):
        return pltpu.make_async_copy(src, dst, sem)

    def drain(ref, sem):
        pltpu.make_async_copy(ref, ref, sem).wait()

    bar = pltpu.get_barrier_semaphore()

    @pl.loop(1, nz)
    def _(k):
        pl.semaphore_signal(bar, inc=1, device_id=zdev(k), device_id_type=MESH)

    @pl.loop(1, nq)
    def _(k):
        pl.semaphore_signal(bar, inc=1, device_id=qdev(qmod(p + k)), device_id_type=MESH)

    pl.semaphore_signal(bar, inc=1, device_id=pdev, device_id_type=MESH)

    loads = [local(a, b, ld.at[i]) for i, (a, b) in enumerate((
        (gate_hbm, gate_v), (up_hbm, up_v), (cot_hbm, cot_v),
        (w_hbm.at[pl.ds(mine, dw_h)], wm.at[pl.ds(0, dw_h)]),
        (w_hbm.at[pl.ds(other, dw_h)], wm.at[pl.ds(dw_h, dw_h)])))]
    for l in loads:
        l.start()
    loads[0].wait()
    loads[1].wait()
    g = gate_v[...].astype(F32)
    hall[0] = (g / (1.0 + jnp.exp(-g)) * up_v[...].astype(F32)).astype(BF16)
    for l in loads[2:]:
        l.wait()
    br, bc = mask_ref.shape
    bs = dr // br
    for i in range(br):
        row = lax.rem(c * (br // 2) + i, br)
        for j in range(bc):
            sl = (pl.ds(i * bs, bs), pl.ds(j * bs, bs))
            keep = jnp.full((bs, bs), mask_ref[row, j], jnp.int32) > 0
            wm[sl] = jnp.where(keep, wm[sl], jnp.zeros((bs, bs), BF16))
    pl.semaphore_wait(bar, nz + nq - 1)

    def steps_of(d, u):
        return half if (u < SUB // 2) == (d == 0) else half - 1

    pairs = [(d, u, 1 - 2 * d, steps_of(d, u)) for u in range(SUB) for d in range(2)]

    def sub(u):
        return pl.ds(u * rsub, rsub)

    def held(d, s):
        return s * 2 - 1 + d

    def ag(d, u, sg, s, src=None, dst=None):
        src = held(d, s) if src is None else src
        dst = held(d, s + 1) if dst is None else dst
        return remote(hall.at[src, sub(u)], hall.at[dst, sub(u)], ag_s, ag_r.at[d, u, s], zdev(sg))

    def y_send(i, k):
        remote(ysend.at[pl.ds(i, k)], yprt.at[pl.ds(i, k)], yp_s, yp_r.at[i], pdev).start()

    def y_dot(i, k):
        v = nt_dot(hall[pl.ds(i, k)].reshape(k * tok, ffc), wm[...])
        ysend[pl.ds(i, k)] = v[:, dw_h:].astype(BF16).reshape(k, tok, dw_h)
        yown[pl.ds(i, k)] = v[:, :dw_h].reshape(k, tok, dw_h)
        y_send(i, k)

    def y_add(i, k):
        rows = pl.ds(i, k)
        drain(yprt.at[rows], yp_r.at[i])
        ysum[rows] = (yown[rows] + yprt[rows].astype(F32)).astype(BF16)

    def y_scatter(n):
        lo, hi = grps[n]
        rows = pl.ds(lo, hi - lo)
        local(ysum.at[(rows,) + tile(p)], yrecv.at[p, rows], yr_r.at[n]).start()

        @pl.loop(1, nq)
        def _(k):
            q = qmod(p + k)
            remote(ysum.at[(rows,) + tile(q)], yrecv.at[p, rows], yr_s, yr_r.at[n], qdev(q)).start()

    def y_finish(n):
        lo, hi = grps[n]
        rows = pl.ds(lo, hi - lo)
        drain(yrecv.at[:, rows], yr_r.at[n])
        osum[rows] = jnp.sum(yrecv[:, rows].astype(F32), axis=0).astype(BF16)
        for i in range(lo, hi):
            if i == 0:
                local(osum.at[0], oB.at[z], oB_r).start()
            else:
                off = -((i + 1) // 2) if i % 2 else i // 2
                remote(osum.at[i], oB.at[z], oB_s, oB_r, zdev(off)).start()

    def cot_one():
        local(cot_v.at[tile(p)], cA.at[p], cA_r).start()

        @pl.loop(1, nq)
        def _(k):
            q = qmod(p + k)
            remote(cot_v.at[tile(q)], cA.at[p], cA_s, cA_r, qdev(q)).start()

    near = nz // 2

    def cot_two():
        drain(cA, cA_r)
        local(cA.at[z], cB.at[0], cB_r.at[0]).start()

        def to(k, idx):
            dev = zdev(k)
            remote(cA.at[dev[0]], cB.at[idx], cB_s, cB_r.at[lax.div(idx, near)], dev).start()

        @pl.loop(1, half)
        def _(m):
            to(m, 2 * m - 1)
            to(-m, 2 * m)

        dev = zdev(half)
        remote(cA.at[dev[0]], cB.at[nz - 1], cB_s, cB_r.at[1], dev).start()

    def cot_three(n):
        rows = pl.ds(n * near, near)
        drain(cB.at[rows], cB_r.at[n])
        dst = call.at[(rows,) + tile(p)]
        local(cB.at[rows], dst, cg_r.at[n]).start()

        @pl.loop(1, nq)
        def _(k):
            remote(cB.at[rows], dst, cg_s, cg_r.at[n], qdev(qmod(p + k))).start()

    def cot_pass(n):
        rows = pl.ds(n * near, near)
        ref = call.at[rows, :, pl.ds(0, dw_h)]
        drain(ref, cg_r.at[n])
        remote(ref, call.at[rows, :, pl.ds(dw_h, dw_h)], rel_s, rel_r.at[n], pdev).start()

    def cot_have(n):
        drain(call.at[pl.ds(n * near, near), :, pl.ds(dw_h, dw_h)], rel_r.at[n])

    for d, u, sg, n in pairs:
        ag(d, u, sg, 0, src=0).start()
    cot_one()
    y_dot(0, 1)

    def ag_step(s, u_static, events):
        for d, u, sg, n in pairs:
            drain(hall.at[held(d, s), sub(u)], ag_r.at[d, u, s - 1])
            if u_static is None:
                ag(d, u, sg, s).start()
            elif n == half:
                ag(d, u, sg, s, dst=nz - 1).start()
            if u == SUB // 2 - 1 and d == 1:
                if u_static is not None and half == 2:
                    y_add(0, 1)
                elif u_static is not None:
                    y_add(2 * s - 3, 2)
                else:
                    @pl.when(s == 1)
                    def _():
                        y_add(0, 1)

                    @pl.when(s > 1)
                    def _():
                        y_add(2 * s - 3, 2)
                for at, fn in events:
                    if u_static is None:
                        pl.when(s == at)(fn)
                    elif at >= u_static:
                        fn()
        y_dot(2 * s - 1, 2)

    if big:
        events = [(2, cot_two), (4, functools.partial(cot_three, 0)), (5, functools.partial(cot_three, 1)),
                  (5, functools.partial(y_scatter, 0)), (6, functools.partial(y_scatter, 1)),
                  (7, functools.partial(cot_pass, 0))]
    else:
        events = [(7, cot_two), (7, functools.partial(cot_three, 0)), (7, functools.partial(cot_three, 1)),
                  (7, functools.partial(cot_pass, 0))]

    @pl.loop(1, half - 1)
    def _(s):
        ag_step(s, None, events)

    ag_step(half - 1, half - 1, events)
    cot_pass(1)
    for d, u, sg, n in pairs:
        if n == half:
            drain(hall.at[nz - 1, sub(u)], ag_r.at[d, u, half - 1])
    y_dot(nz - 1, 1)
    y_add(nz - 3, 2)
    cot_have(0)
    cot_have(1)

    def rs(d, u, sg, s):
        return remote(sbuf.at[d, s, sub(u)], rbuf.at[d, s, sub(u)], rs_s, rs_r.at[d, u, s], zdev(sg))

    def part(s, buf):
        m = half - s
        v = jnp.dot(call[pl.ds(2 * m - 1, 2)].reshape(2 * tok, dr), wm[...], preferred_element_type=F32)
        pbuf[buf] = v.reshape(2, tok, ffc)

    def part_one(i):
        pbuf[0, 0] = jnp.dot(call[i], wm[...], preferred_element_type=F32)

    def dw(n):
        lo, hi = n * nz // 4, (n + 1) * nz // 4
        v = tn_dot(call[lo:hi].reshape((hi - lo) * tok, dr), hall[lo:hi].reshape((hi - lo) * tok, ffc))
        if n == 0:
            acc[...] = v
        elif n < 3:
            acc[...] += v
        else:
            accb[...] = (acc[...] + v).astype(BF16)
            local(accb.at[pl.ds(0, dw_h)], dw_hbm.at[pl.ds(mine, dw_h)], st.at[0]).start()
            local(accb.at[pl.ds(dw_h, dw_h)], dw_hbm.at[pl.ds(other, dw_h)], st.at[1]).start()

    part_one(nz - 1)
    for d, u, sg, n in pairs:
        if n == half:
            sbuf[d, 0, sub(u)] = pbuf[0, 0, sub(u)].astype(BF16)
    for d, u, sg, n in pairs:
        if n == half:
            rs(d, u, sg, 0).start()
    part(1, 1)
    for d, u, sg, n in pairs:
        if n < half:
            sbuf[d, 1, sub(u)] = pbuf[1, 1 - d, sub(u)].astype(BF16)
    for d, u, sg, n in pairs:
        if n < half:
            rs(d, u, sg, 1).start()
    y_add(nz - 1, 1)
    for n in range(2 if big else 0, len(grps)):
        y_scatter(n)
    dw(0)

    def out_two():
        drain(oB, oB_r)
        local(oB.at[p], out_v.at[tile(p)], ov_r).start()

        @pl.loop(1, nq)
        def _(k):
            q = qmod(p + k)
            remote(oB.at[q], out_v.at[tile(p)], ov_s, ov_r, qdev(q)).start()

    if big:
        mids = [(1, functools.partial(dw, 1)), (2, functools.partial(dw, 2)), (3, functools.partial(dw, 3)),
                (2, functools.partial(y_finish, 0)), (3, functools.partial(y_finish, 1)),
                (4, functools.partial(y_finish, 2)), (4, functools.partial(y_finish, 3)), (7, out_two)]
    else:
        mids = [(1, functools.partial(dw, n)) for n in (1, 2, 3)]
        mids += [(1, functools.partial(y_finish, n)) for n in range(len(grps))] + [(1, out_two)]

    def rs_add(d, u, s):
        drain(rbuf.at[d, s - 1, sub(u)], rs_r.at[d, u, s - 1])
        sbuf[d, s, sub(u)] = (pbuf[lax.rem(s, 2), 1 - d, sub(u)]
                              + rbuf[d, s - 1, sub(u)].astype(F32)).astype(BF16)

    @pl.loop(1, half)
    def _(s):
        for d, u, sg, n in pairs:
            if n == half:
                rs_add(d, u, s)
                rs(d, u, sg, s).start()
            else:
                @pl.when(s > 1)
                def _():
                    rs_add(d, u, s)
                    rs(d, u, sg, s).start()
            if u == SUB // 2 - 1 and d == 1:
                @pl.when(s < half - 1)
                def _():
                    part(s + 1, lax.rem(s + 1, 2))
        for at, fn in mids:
            pl.when(s == at)(fn)

    part_one(0)
    for d, u, sg, n in pairs:
        drain(rbuf.at[d, half - 1, sub(u)], rs_r.at[d, u, half - 1])
        if d == 1:
            pbuf[0, 0, sub(u)] += (rbuf[0, half - 1, sub(u)].astype(F32)
                                   + rbuf[1, half - 1, sub(u)].astype(F32))
    local(pbuf.at[0, 0], dh_hbm, st.at[2]).start()
    drain(out_v, ov_r)
    local(out_v, out_hbm, st.at[3]).start()

    most = pl.ds(0, nz - 1)
    rest = pl.ds(0, nq - 1)
    drain(hall.at[most], ag_s)
    drain(hall.at[most], rs_s)
    drain(cA.at[rest], cA_s)
    drain(cB.at[most], cB_s)
    drain(call.at[rest, :, pl.ds(0, dw_h)], cg_s)
    drain(call.at[:, :, pl.ds(0, dw_h)], rel_s)
    drain(ysend, yp_s)
    drain(yrecv.at[rest], yr_s)
    drain(oB.at[most], oB_s)
    drain(oB.at[rest], ov_s)
    drain(accb.at[pl.ds(0, dw_h)], st.at[0])
    drain(accb.at[pl.ds(0, dw_h)], st.at[1])
    local(pbuf.at[0, 0], dh_hbm, st.at[2]).wait()
    local(out_v, out_hbm, st.at[3]).wait()


def finish(gate_ref, up_ref, mask_ref, outr_ref, dh_ref, dw_ref, out_ref, dgate_ref, dup_ref, ddown_ref):
    tok = gate_ref.shape[0]
    for r in range(0, tok, 32):
        rows = pl.ds(r, 32)
        dh = dh_ref[rows, :]
        g = gate_ref[rows, :].astype(F32)
        sig = 1.0 / (1.0 + jnp.exp(-g))
        dgate_ref[rows, :] = (dh * up_ref[rows, :].astype(F32) * sig * (1.0 + g * (1.0 - sig))).astype(BF16)
        dup_ref[rows, :] = (dh * (g * sig)).astype(BF16)
    br, bc = mask_ref.shape
    bs = dw_ref.shape[0] // br
    for i in range(br):
        for j in range(bc):
            sl = (pl.ds(i * bs, bs), pl.ds(j * bs, bs))
            keep = jnp.full((bs, bs), mask_ref[i, j], jnp.int32) > 0
            ddown_ref[sl] = jnp.where(keep, dw_ref[sl], jnp.zeros((bs, bs), BF16))
    out_ref[...] = outr_ref[...]


def body(nz, nq, gate_pre, up_pre, down_weight, block_mask, cotangent):
    tok, ffc = gate_pre.shape
    dr = down_weight.shape[0]
    dw_h = dr // 2
    half = nz // 2
    ng = len(groups(nz))
    dma = pltpu.SemaphoreType.DMA
    vm = pltpu.VMEM
    any_ = pl.BlockSpec(memory_space=pl.ANY)
    vmem = pl.BlockSpec(memory_space=pltpu.VMEM)
    smem = pl.BlockSpec(memory_space=pltpu.SMEM)
    outr, dh, dwr = pl.pallas_call(
        functools.partial(kernel, nz, nq),
        out_shape=(
            jax.ShapeDtypeStruct((tok, dw_h), BF16),
            jax.ShapeDtypeStruct((tok, ffc), F32),
            jax.ShapeDtypeStruct((dr, ffc), BF16),
        ),
        in_specs=[any_, any_, any_, smem, any_],
        out_specs=(any_,) * 3,
        scratch_shapes=[
            vm((tok, ffc), BF16), vm((tok, ffc), BF16), vm((dr, ffc), BF16), vm((tok, dw_h), BF16),
            vm((nz, tok, ffc), BF16), vm((nz, tok, dr), BF16),
            vm((nq, TR, TC), BF16), vm((nz, TR, TC), BF16),
            vm((nz, tok, dw_h), F32), vm((nz, tok, dw_h), BF16), vm((nz, tok, dw_h), BF16),
            vm((nz, tok, dw_h), BF16), vm((nq, nz, TR, TC), BF16),
            vm((nz, TR, TC), BF16), vm((nz, TR, TC), BF16), vm((tok, dw_h), BF16),
            vm((2, half, tok, ffc), BF16), vm((2, half, tok, ffc), BF16),
            vm((2, 2, tok, ffc), F32), vm((dr, ffc), F32), vm((dr, ffc), BF16),
            dma((5,)), dma, dma((2, SUB, half)), dma, dma((2, SUB, half)),
            dma, dma, dma, dma((2,)),
            dma, dma((2,)), dma, dma((2,)), dma, dma((nz,)), dma, dma((ng,)),
            dma, dma, dma, dma, dma((4,)),
        ],
        compiler_params=pltpu.CompilerParams(
            collective_id=0, has_side_effects=True, vmem_limit_bytes=60 * 1024 * 1024),
    )(gate_pre, up_pre, down_weight, block_mask, cotangent)
    return pl.pallas_call(
        finish,
        out_shape=(
            jax.ShapeDtypeStruct((tok, dw_h), BF16),
            jax.ShapeDtypeStruct((tok, ffc), BF16),
            jax.ShapeDtypeStruct((tok, ffc), BF16),
            jax.ShapeDtypeStruct((dr, ffc), BF16),
        ),
        in_specs=[vmem, vmem, smem, vmem, vmem, vmem],
        out_specs=(vmem,) * 4,
    )(gate_pre, up_pre, block_mask, outr, dh, dwr)


def solution(mesh):
    nz = mesh.shape["row"]
    nq = mesh.shape["col"] // 2
    spec = P("row", "col")
    return jax.shard_map(functools.partial(body, nz, nq), mesh=mesh, in_specs=(spec,) * 5,
                         out_specs=(spec,) * 4, check_vma=False)
```

time: 471 us -> 89.8 us (0.19)
  waiting for transfers between devices: 405 us -> 0 us
  Pallas kernels: 0 us -> 87.9 us
  local copies, waits for them, and re-layouts: 20.3 us -> 0 us
  matrix products: 16.1 us -> 0 us
  between operations: 13.8 us -> 0.64 us
  starting transfers between devices: 12.4 us -> 0 us
    all_gather x3 -> x0, waiting for transfers between devices: 307 us -> none  [the longest x1 179 us: body(): panel = lax.all_gather(masked, 'row', axis=0, tiled=True)]
    reduce_scatter x1 -> x0, waiting for transfers between devices: 97.5 us -> none  [body(): lax.psum_scatter(y_summand.astype(jnp.bfloat16), 'col', scatter_dimension...]
    pallas_call x0 -> x2, Pallas kernels: none -> 87.9 us  [the longest x1 85.5 us: body(): pl.pallas_call(functools.partial(kernel, nz, nq), out_shape=(jax.ShapeDty...]
    dot_general x3 -> x0, matrix products: 16.1 us -> none  [the longest x1 6.49 us: body(): jnp.einsum('tnd,ndf->ntf', cot_row.reshape(tok_rows, shards, d_rows), pan...]
    all_to_all x1 -> x0, starting transfers between devices: 12.3 us -> none  [body(): lax.all_to_all(cot_row, 'row', split_axis=1, concat_axis=0, tiled=True)]
    all_gather x1 -> x0, local copies, waits for them, and re-layouts: 11.9 us -> none  [body(): panel = lax.all_gather(masked, 'row', axis=0, tiled=True)]
    unnamed x13 -> x0, local copies, waits for them, and re-layouts: 5.76 us -> none
  transfers between devices with their start and end apart: 5 -> 0, of which waited for: 4 -> 0; matrix products, arithmetic and copies ran while one was open for 8% -> 0% of each run, Pallas kernels for 0% -> 0%
where the time goes in v2:
time: 89.8 us; the launch traced here: 88.5 us
  Pallas kernels  87.9 us (98%)
    pallas_call x1, Pallas kernels, body(): pl.pallas_call(functools.partial(kernel, nz, nq), out_shape=(jax.ShapeDty...  85.5 us
    pallas_call x1, Pallas kernels, body(): pl.pallas_call(finish, out_shape=(jax.ShapeDtypeStruct((tok, dw_h), BF16)...  2.34 us

profile of v2, /device:TPU:6, one launch (start us, length us, event | category | flops | bytes accessed | tf_op | source)
XLA Modules:
  0.0 88.5 jit_solution(12868355522413702422)
XLA Ops:
  0.6 85.5 %shard_map.84 = (bf16[128,256]{1,0:T(8,128)(2,1)}, f32[128,512]{1,0:T(8,128)}, bf16[512,512]{1,0:T(8,128)(2,1)}) custom-call(bf16[128,512]{1,0:T(8,128)(2,1)} %gate_ref.1, bf16[128,512]{1,0:T(8,128)(2,1)} %up_ref.1, bf16[512,512]{1,0:T(8,128)(2,1)} %w_hbm.1, s32[4,4]{1,0:T(4,128)} %mask_ref.3, bf16[128,256]{1,0:T(8,128)(2,1)} %cot_hbm.1), custom_call_target="tpu_custom_call" | custom-call | tf_op jit(solution)/shard_map/pallas_call | solution.py:407
  86.2 2.3 %shard_map.85 = (bf16[128,256]{1,0:T(8,128)(2,1)}, bf16[128,512]{1,0:T(8,128)(2,1)}, bf16[128,512]{1,0:T(8,128)(2,1)}, bf16[512,512]{1,0:T(8,128)(2,1)}) custom-call(bf16[128,512]{1,0:T(8,128)(2,1)} %gate_ref.1, bf16[128,512]{1,0:T(8,128)(2,1)} %up_ref.1, s32[4,4]{1,0:T(4,128)} %mask_ref.3, bf16[128,256]{1,0:T(8,128)(2,1)} %get-tuple-element.7.outr_ref, ...), custom_call_target="tpu_custom_call" | custom-call | tf_op jit(solution)/shard_map/pallas_call | solution.py:433

commit v3 on v2

--- a/solution.py
+++ b/solution.py
@@ -27,8 +27,15 @@
     half = nz // 2
     if half <= 4:
         return [(i, i + 1) for i in range(nz)]
-    cut = [0, 5, 9, 13, nz]
+    cut = [0, half - 3, nz - 5, nz]
     return list(zip(cut[:-1], cut[1:]))
+
+
+def cot_groups(nz):
+    half = nz // 2
+    if half <= 4:
+        return [(0, 1), (1, 2), (2, nz)]
+    return [(0, half - 1), (half - 1, nz - 3), (nz - 3, nz)]
 
 
 def kernel(nz, nq, gate_hbm, up_hbm, w_hbm, mask_ref, cot_hbm,
@@ -50,6 +57,7 @@
     rsub = tok // SUB
     big = half > 4
     grps = groups(nz)
+    cgrps = cot_groups(nz)
 
     def zdev(k):
         return (lax.rem(z + (k + nz), nz), col)
@@ -173,26 +181,20 @@
             q = qmod(p + k)
             remote(cot_v.at[tile(q)], cA.at[p], cA_s, cA_r, qdev(q)).start()
 
-    near = nz // 2
+    def crows(n):
+        return pl.ds(cgrps[n][0], cgrps[n][1] - cgrps[n][0])
 
     def cot_two():
         drain(cA, cA_r)
         local(cA.at[z], cB.at[0], cB_r.at[0]).start()
-
-        def to(k, idx):
+        for i in range(nz - 1, 0, -1):
+            k = (i + 1) // 2 if i % 2 else -(i // 2)
+            n = [lo <= i < hi for lo, hi in cgrps].index(True)
             dev = zdev(k)
-            remote(cA.at[dev[0]], cB.at[idx], cB_s, cB_r.at[lax.div(idx, near)], dev).start()
-
-        @pl.loop(1, half)
-        def _(m):
-            to(m, 2 * m - 1)
-            to(-m, 2 * m)
-
-        dev = zdev(half)
-        remote(cA.at[dev[0]], cB.at[nz - 1], cB_s, cB_r.at[1], dev).start()
+            remote(cA.at[dev[0]], cB.at[i], cB_s, cB_r.at[n], dev).start()
 
     def cot_three(n):
-        rows = pl.ds(n * near, near)
+        rows = crows(n)
         drain(cB.at[rows], cB_r.at[n])
         dst = call.at[(rows,) + tile(p)]
         local(cB.at[rows], dst, cg_r.at[n]).start()
@@ -202,67 +204,56 @@
             remote(cB.at[rows], dst, cg_s, cg_r.at[n], qdev(qmod(p + k))).start()
 
     def cot_pass(n):
-        rows = pl.ds(n * near, near)
-        ref = call.at[rows, :, pl.ds(0, dw_h)]
+        ref = call.at[crows(n), :, pl.ds(0, dw_h)]
         drain(ref, cg_r.at[n])
-        remote(ref, call.at[rows, :, pl.ds(dw_h, dw_h)], rel_s, rel_r.at[n], pdev).start()
+        remote(ref, call.at[crows(n), :, pl.ds(dw_h, dw_h)], rel_s, rel_r.at[n], pdev).start()
 
     def cot_have(n):
-        drain(call.at[pl.ds(n * near, near), :, pl.ds(dw_h, dw_h)], rel_r.at[n])
-
+        drain(call.at[crows(n), :, pl.ds(dw_h, dw_h)], rel_r.at[n])
+
+    def ag_far(d, u, sg, src):
+        remote(hall.at[src, sub(u)], hall.at[nz - 1, sub(u)], ag_s, ag_r.at[d, u, half - 1], zdev(2 * sg)).start()
+
+    cot_one()
     for d, u, sg, n in pairs:
         ag(d, u, sg, 0, src=0).start()
-    cot_one()
+        if half == 2 and n == half:
+            ag_far(d, u, sg, 0)
     y_dot(0, 1)
 
-    def ag_step(s, u_static, events):
+    near, mid, far = 0, 1, 2
+    events = [(1, cot_two), (3, functools.partial(cot_three, near)), (4, functools.partial(cot_three, far)),
+              (4, functools.partial(cot_three, mid)), (5, functools.partial(y_scatter, 0)),
+              (6, functools.partial(cot_pass, near)), (6, functools.partial(cot_pass, far))]
+
+    @pl.loop(1, half - 1)
+    def _(s):
         for d, u, sg, n in pairs:
             drain(hall.at[held(d, s), sub(u)], ag_r.at[d, u, s - 1])
-            if u_static is None:
-                ag(d, u, sg, s).start()
-            elif n == half:
-                ag(d, u, sg, s, dst=nz - 1).start()
-            if u == SUB // 2 - 1 and d == 1:
-                if u_static is not None and half == 2:
+            ag(d, u, sg, s).start()
+            if n == half:
+                @pl.when(s == half - 2)
+                def _():
+                    ag_far(d, u, sg, held(d, s))
+            if u == 0 and d == 1:
+                @pl.when(s == 1)
+                def _():
                     y_add(0, 1)
-                elif u_static is not None:
+
+                @pl.when(s > 1)
+                def _():
                     y_add(2 * s - 3, 2)
-                else:
-                    @pl.when(s == 1)
-                    def _():
-                        y_add(0, 1)
-
-                    @pl.when(s > 1)
-                    def _():
-                        y_add(2 * s - 3, 2)
-                for at, fn in events:
-                    if u_static is None:
-                        pl.when(s == at)(fn)
-                    elif at >= u_static:
-                        fn()
         y_dot(2 * s - 1, 2)
-
-    if big:
-        events = [(2, cot_two), (4, functools.partial(cot_three, 0)), (5, functools.partial(cot_three, 1)),
-                  (5, functools.partial(y_scatter, 0)), (6, functools.partial(y_scatter, 1)),
-                  (7, functools.partial(cot_pass, 0))]
-    else:
-        events = [(7, cot_two), (7, functools.partial(cot_three, 0)), (7, functools.partial(cot_three, 1)),
-                  (7, functools.partial(cot_pass, 0))]
-
-    @pl.loop(1, half - 1)
-    def _(s):
-        ag_step(s, None, events)
-
-    ag_step(half - 1, half - 1, events)
-    cot_pass(1)
-    for d, u, sg, n in pairs:
-        if n == half:
-            drain(hall.at[nz - 1, sub(u)], ag_r.at[d, u, half - 1])
-    y_dot(nz - 1, 1)
-    y_add(nz - 3, 2)
-    cot_have(0)
-    cot_have(1)
+        for at, fn in events:
+            pl.when(s == at)(fn)
+
+    if not big:
+        for at, fn in events:
+            if fn is not events[4][1]:
+                fn()
+    for d, u, sg, n in pairs:
+        drain(hall.at[held(d, half - 1), sub(u)], ag_r.at[d, u, half - 2])
+    cot_have(far)
 
     def rs(d, u, sg, s):
         return remote(sbuf.at[d, s, sub(u)], rbuf.at[d, s, sub(u)], rs_s, rs_r.at[d, u, s], zdev(sg))
@@ -287,24 +278,44 @@
             local(accb.at[pl.ds(0, dw_h)], dw_hbm.at[pl.ds(mine, dw_h)], st.at[0]).start()
             local(accb.at[pl.ds(dw_h, dw_h)], dw_hbm.at[pl.ds(other, dw_h)], st.at[1]).start()
 
+    if not big:
+        cot_pass(mid)
+        cot_have(mid)
+        cot_have(near)
     part_one(nz - 1)
     for d, u, sg, n in pairs:
         if n == half:
             sbuf[d, 0, sub(u)] = pbuf[0, 0, sub(u)].astype(BF16)
+            remote(sbuf.at[d, 0, sub(u)], rbuf.at[d, 0, sub(u)], rs_s, rs_r.at[d, u, 0], zdev(2 * sg)).start()
+    part(1, 1)
+    for d, u, sg, n in pairs:
+        sbuf[d, 1, sub(u)] = pbuf[1, 1 - d, sub(u)].astype(BF16)
+        rs(d, u, sg, 1).start()
+    if big:
+        cot_pass(mid)
+        y_add(nz - 5, 2)
+        y_scatter(1)
+        y_dot(nz - 3, 2)
+    else:
+        y_add(0, 1)
+        y_dot(1, 2)
     for d, u, sg, n in pairs:
         if n == half:
-            rs(d, u, sg, 0).start()
-    part(1, 1)
-    for d, u, sg, n in pairs:
-        if n < half:
-            sbuf[d, 1, sub(u)] = pbuf[1, 1 - d, sub(u)].astype(BF16)
-    for d, u, sg, n in pairs:
-        if n < half:
-            rs(d, u, sg, 1).start()
+            drain(hall.at[nz - 1, sub(u)], ag_r.at[d, u, half - 1])
+    y_dot(nz - 1, 1)
+    y_add(nz - 3, 2)
+    if big:
+        cot_have(mid)
+        part(2, 0)
     y_add(nz - 1, 1)
-    for n in range(2 if big else 0, len(grps)):
-        y_scatter(n)
-    dw(0)
+    if big:
+        y_scatter(2)
+        cot_have(near)
+    else:
+        for n in range(len(grps)):
+            y_scatter(n)
+        for n in range(4):
+            dw(n)
 
     def out_two():
         drain(oB, oB_r)
@@ -315,30 +326,30 @@
             q = qmod(p + k)
             remote(oB.at[q], out_v.at[tile(p)], ov_s, ov_r, qdev(q)).start()
 
-    if big:
-        mids = [(1, functools.partial(dw, 1)), (2, functools.partial(dw, 2)), (3, functools.partial(dw, 3)),
-                (2, functools.partial(y_finish, 0)), (3, functools.partial(y_finish, 1)),
-                (4, functools.partial(y_finish, 2)), (4, functools.partial(y_finish, 3)), (7, out_two)]
-    else:
-        mids = [(1, functools.partial(dw, n)) for n in (1, 2, 3)]
-        mids += [(1, functools.partial(y_finish, n)) for n in range(len(grps))] + [(1, out_two)]
+    mids = [(2, functools.partial(y_finish, 0)), (2, functools.partial(y_finish, 1)),
+            (3, functools.partial(y_finish, 2)), (4, functools.partial(dw, 0)), (4, functools.partial(dw, 1)),
+            (5, functools.partial(dw, 2)), (5, functools.partial(dw, 3)), (6, out_two)]
+    if not big:
+        for n in range(len(grps)):
+            y_finish(n)
+        out_two()
 
     def rs_add(d, u, s):
         drain(rbuf.at[d, s - 1, sub(u)], rs_r.at[d, u, s - 1])
         sbuf[d, s, sub(u)] = (pbuf[lax.rem(s, 2), 1 - d, sub(u)]
                               + rbuf[d, s - 1, sub(u)].astype(F32)).astype(BF16)
 
-    @pl.loop(1, half)
+    @pl.loop(2, half)
     def _(s):
         for d, u, sg, n in pairs:
             if n == half:
-                rs_add(d, u, s)
-                rs(d, u, sg, s).start()
-            else:
-                @pl.when(s > 1)
+                @pl.when(s == 2)
                 def _():
-                    rs_add(d, u, s)
-                    rs(d, u, sg, s).start()
+                    drain(rbuf.at[d, 0, sub(u)], rs_r.at[d, u, 0])
+                    pbuf[0, 1 - d, sub(u)] += rbuf[d, 0, sub(u)].astype(F32)
+
+            rs_add(d, u, s)
+            rs(d, u, sg, s).start()
             if u == SUB // 2 - 1 and d == 1:
                 @pl.when(s < half - 1)
                 def _():
@@ -349,6 +360,9 @@
     part_one(0)
     for d, u, sg, n in pairs:
         drain(rbuf.at[d, half - 1, sub(u)], rs_r.at[d, u, half - 1])
+        if half == 2 and n == half:
+            drain(rbuf.at[d, 0, sub(u)], rs_r.at[d, u, 0])
+            pbuf[0, 0, sub(u)] += rbuf[d, 0, sub(u)].astype(F32)
         if d == 1:
             pbuf[0, 0, sub(u)] += (rbuf[0, half - 1, sub(u)].astype(F32)
                                    + rbuf[1, half - 1, sub(u)].astype(F32))
@@ -423,8 +437,8 @@
             vm((2, half, tok, ffc), BF16), vm((2, half, tok, ffc), BF16),
             vm((2, 2, tok, ffc), F32), vm((dr, ffc), F32), vm((dr, ffc), BF16),
             dma((5,)), dma, dma((2, SUB, half)), dma, dma((2, SUB, half)),
-            dma, dma, dma, dma((2,)),
-            dma, dma((2,)), dma, dma((2,)), dma, dma((nz,)), dma, dma((ng,)),
+            dma, dma, dma, dma((3,)),
+            dma, dma((3,)), dma, dma((3,)), dma, dma((nz,)), dma, dma((ng,)),
             dma, dma, dma, dma, dma((4,)),
         ],
         compiler_params=pltpu.CompilerParams(

time: 89.8 us -> 82 us (0.913); the launches traced: 88.5 us -> 81.9 us
  Pallas kernels: 87.9 us -> 81.2 us
    pallas_call x1, Pallas kernels: 85.5 us -> 78.9 us  [body(): pl.pallas_call(functools.partial(kernel, nz, nq), out_shape=(jax.ShapeDty...]
where the time goes in v3:
time: 82 us; the launch traced here: 81.9 us
  Pallas kernels  81.2 us (99%)
    pallas_call x1, Pallas kernels, body(): pl.pallas_call(functools.partial(kernel, nz, nq), out_shape=(jax.ShapeDty...  78.9 us
    pallas_call x1, Pallas kernels, body(): pl.pallas_call(finish, out_shape=(jax.ShapeDtypeStruct((tok, dw_h), BF16)...  2.34 us

profile of v3, /device:TPU:6, one launch (start us, length us, event | category | flops | bytes accessed | tf_op | source)
XLA Modules:
  0.0 81.9 jit_solution(10894843803225525497)
XLA Ops:
  0.6 78.9 %shard_map.84 = (bf16[128,256]{1,0:T(8,128)(2,1)}, f32[128,512]{1,0:T(8,128)}, bf16[512,512]{1,0:T(8,128)(2,1)}) custom-call(bf16[128,512]{1,0:T(8,128)(2,1)} %gate_ref.1, bf16[128,512]{1,0:T(8,128)(2,1)} %up_ref.1, bf16[512,512]{1,0:T(8,128)(2,1)} %w_hbm.1, s32[4,4]{1,0:T(4,128)} %mask_ref.3, bf16[128,256]{1,0:T(8,128)(2,1)} %cot_hbm.1), custom_call_target="tpu_custom_call" | custom-call | tf_op jit(solution)/shard_map/pallas_call | solution.py:421
  79.5 2.3 %shard_map.85 = (bf16[128,256]{1,0:T(8,128)(2,1)}, bf16[128,512]{1,0:T(8,128)(2,1)}, bf16[128,512]{1,0:T(8,128)(2,1)}, bf16[512,512]{1,0:T(8,128)(2,1)}) custom-call(bf16[128,512]{1,0:T(8,128)(2,1)} %gate_ref.1, bf16[128,512]{1,0:T(8,128)(2,1)} %up_ref.1, s32[4,4]{1,0:T(4,128)} %mask_ref.3, bf16[128,256]{1,0:T(8,128)(2,1)} %get-tuple-element.7.outr_ref, ...), custom_call_target="tpu_custom_call" | custom-call | tf_op jit(solution)/shard_map/pallas_call | solution.py:447

commit v4 on v3

--- a/solution.py
+++ b/solution.py
@@ -27,7 +27,7 @@
     half = nz // 2
     if half <= 4:
         return [(i, i + 1) for i in range(nz)]
-    cut = [0, half - 3, nz - 5, nz]
+    cut = [0, 3, nz - 5, nz]
     return list(zip(cut[:-1], cut[1:]))
 
 
@@ -45,7 +45,7 @@
            rbuf, sbuf, pbuf, acc, accb,
            ld, ag_s, ag_r, rs_s, rs_r, cA_s, cA_r, cB_s, cB_r,
            cg_s, cg_r, rel_s, rel_r, yp_s, yp_r, yr_s, yr_r,
-           oB_s, oB_r, ov_s, ov_r, st):
+           oB_s, oB_r, ov_s, ov_r, st, far_sem):
     z = lax.axis_index("row")
     col = lax.axis_index("col")
     p = lax.div(col, 2)
@@ -89,8 +89,8 @@
 
     bar = pltpu.get_barrier_semaphore()
 
-    @pl.loop(1, nz)
-    def _(k):
+    near_z = (1, -1, 2, -2) if big else range(1, nz)
+    for k in near_z:
         pl.semaphore_signal(bar, inc=1, device_id=zdev(k), device_id_type=MESH)
 
     @pl.loop(1, nq)
@@ -119,7 +119,17 @@
             sl = (pl.ds(i * bs, bs), pl.ds(j * bs, bs))
             keep = jnp.full((bs, bs), mask_ref[row, j], jnp.int32) > 0
             wm[sl] = jnp.where(keep, wm[sl], jnp.zeros((bs, bs), BF16))
-    pl.semaphore_wait(bar, nz + nq - 1)
+    pl.semaphore_wait(bar, len(near_z) + nq)
+
+    def tell(n):
+        for k in (2 << n, -(2 << n)):
+            pl.semaphore_signal(far_sem.at[n], inc=1, device_id=zdev(k), device_id_type=MESH)
+
+    def hear(n):
+        pl.semaphore_wait(far_sem.at[n], 2)
+
+    if big:
+        tell(0)
 
     def steps_of(d, u):
         return half if (u < SUB // 2) == (d == 0) else half - 1
@@ -151,12 +161,13 @@
         drain(yprt.at[rows], yp_r.at[i])
         ysum[rows] = (yown[rows] + yprt[rows].astype(F32)).astype(BF16)
 
-    def y_scatter(n):
+    def y_scatter(n, first=1, end=nq):
         lo, hi = grps[n]
         rows = pl.ds(lo, hi - lo)
-        local(ysum.at[(rows,) + tile(p)], yrecv.at[p, rows], yr_r.at[n]).start()
-
-        @pl.loop(1, nq)
+        if first == 1:
+            local(ysum.at[(rows,) + tile(p)], yrecv.at[p, rows], yr_r.at[n]).start()
+
+        @pl.loop(first, end)
         def _(k):
             q = qmod(p + k)
             remote(ysum.at[(rows,) + tile(q)], yrecv.at[p, rows], yr_s, yr_r.at[n], qdev(q)).start()
@@ -185,6 +196,8 @@
         return pl.ds(cgrps[n][0], cgrps[n][1] - cgrps[n][0])
 
     def cot_two():
+        if big:
+            hear(1)
         drain(cA, cA_r)
         local(cA.at[z], cB.at[0], cB_r.at[0]).start()
         for i in range(nz - 1, 0, -1):
@@ -193,13 +206,14 @@
             dev = zdev(k)
             remote(cA.at[dev[0]], cB.at[i], cB_s, cB_r.at[n], dev).start()
 
-    def cot_three(n):
+    def cot_three(n, lo=1, hi=nq):
         rows = crows(n)
-        drain(cB.at[rows], cB_r.at[n])
         dst = call.at[(rows,) + tile(p)]
-        local(cB.at[rows], dst, cg_r.at[n]).start()
-
-        @pl.loop(1, nq)
+        if lo == 1:
+            drain(cB.at[rows], cB_r.at[n])
+            local(cB.at[rows], dst, cg_r.at[n]).start()
+
+        @pl.loop(lo, hi)
         def _(k):
             remote(cB.at[rows], dst, cg_s, cg_r.at[n], qdev(qmod(p + k))).start()
 
@@ -219,12 +233,22 @@
         ag(d, u, sg, 0, src=0).start()
         if half == 2 and n == half:
             ag_far(d, u, sg, 0)
+    if big:
+        hear(0)
+        tell(1)
     y_dot(0, 1)
 
     near, mid, far = 0, 1, 2
-    events = [(1, cot_two), (3, functools.partial(cot_three, near)), (4, functools.partial(cot_three, far)),
-              (4, functools.partial(cot_three, mid)), (5, functools.partial(y_scatter, 0)),
-              (6, functools.partial(cot_pass, near)), (6, functools.partial(cot_pass, far))]
+    last = SUB - 1
+    cut = nq // 2
+    events = [(1, last, cot_two), (2, last, functools.partial(y_scatter, 0)),
+              (3, last, functools.partial(cot_three, near)),
+              (4, last, functools.partial(cot_three, far)),
+              (5, SUB // 4, functools.partial(cot_three, mid, 1, cut)),
+              (5, SUB // 2, functools.partial(cot_three, mid, cut, nq)),
+              (6, SUB // 4, functools.partial(y_scatter, 1, 1, cut)),
+              (6, SUB // 2, functools.partial(y_scatter, 1, cut, nq)),
+              (6, last, functools.partial(cot_pass, near)), (6, last, functools.partial(cot_pass, far))]
 
     @pl.loop(1, half - 1)
     def _(s):
@@ -243,13 +267,16 @@
                 @pl.when(s > 1)
                 def _():
                     y_add(2 * s - 3, 2)
-        y_dot(2 * s - 1, 2)
-        for at, fn in events:
-            pl.when(s == at)(fn)
+            if d == 1:
+                if u == last:
+                    y_dot(2 * s - 1, 2)
+                for at, on, fn in events:
+                    if on == u:
+                        pl.when(s == at)(fn)
 
     if not big:
-        for at, fn in events:
-            if fn is not events[4][1]:
+        for at, on, fn in events:
+            if getattr(fn, 'func', None) is not y_scatter:
                 fn()
     for d, u, sg, n in pairs:
         drain(hall.at[held(d, half - 1), sub(u)], ag_r.at[d, u, half - 2])
@@ -294,7 +321,6 @@
     if big:
         cot_pass(mid)
         y_add(nz - 5, 2)
-        y_scatter(1)
         y_dot(nz - 3, 2)
     else:
         y_add(0, 1)
@@ -327,8 +353,8 @@
             remote(oB.at[q], out_v.at[tile(p)], ov_s, ov_r, qdev(q)).start()
 
     mids = [(2, functools.partial(y_finish, 0)), (2, functools.partial(y_finish, 1)),
-            (3, functools.partial(y_finish, 2)), (4, functools.partial(dw, 0)), (4, functools.partial(dw, 1)),
-            (5, functools.partial(dw, 2)), (5, functools.partial(dw, 3)), (6, out_two)]
+            (3, functools.partial(y_finish, 2)), (3, functools.partial(dw, 0)), (4, functools.partial(dw, 1)),
+            (4, functools.partial(dw, 2)), (5, functools.partial(dw, 3)), (6, out_two)]
     if not big:
         for n in range(len(grps)):
             y_finish(n)
@@ -350,10 +376,11 @@
 
             rs_add(d, u, s)
             rs(d, u, sg, s).start()
-            if u == SUB // 2 - 1 and d == 1:
-                @pl.when(s < half - 1)
-                def _():
-                    part(s + 1, lax.rem(s + 1, 2))
+
+        @pl.when(s < half - 1)
+        def _():
+            part(s + 1, lax.rem(s + 1, 2))
+
         for at, fn in mids:
             pl.when(s == at)(fn)
 
@@ -439,7 +466,7 @@
             dma((5,)), dma, dma((2, SUB, half)), dma, dma((2, SUB, half)),
             dma, dma, dma, dma((3,)),
             dma, dma((3,)), dma, dma((3,)), dma, dma((nz,)), dma, dma((ng,)),
-            dma, dma, dma, dma, dma((4,)),
+            dma, dma, dma, dma, dma((4,)), pltpu.SemaphoreType.REGULAR((2,)),
         ],
         compiler_params=pltpu.CompilerParams(
             collective_id=0, has_side_effects=True, vmem_limit_bytes=60 * 1024 * 1024),

time: 82 us -> 80 us (0.976)
  Pallas kernels: 81.2 us -> 78.7 us
    pallas_call x1, Pallas kernels: 78.9 us -> 76.3 us  [body(): pl.pallas_call(functools.partial(kernel, nz, nq), out_shape=(jax.ShapeDty...]
where the time goes in v4:
time: 80 us; the launch traced here: 79.3 us
  Pallas kernels  78.7 us (98%)
    pallas_call x1, Pallas kernels, body(): pl.pallas_call(functools.partial(kernel, nz, nq), out_shape=(jax.ShapeDty...  76.3 us
    pallas_call x1, Pallas kernels, body(): pl.pallas_call(finish, out_shape=(jax.ShapeDtypeStruct((tok, dw_h), BF16)...  2.34 us

profile of v4, /device:TPU:6, one launch (start us, length us, event | category | flops | bytes accessed | tf_op | source)
XLA Modules:
  0.0 79.3 jit_solution(4147790528277895908)
XLA Ops:
  0.6 76.3 %shard_map.84 = (bf16[128,256]{1,0:T(8,128)(2,1)}, f32[128,512]{1,0:T(8,128)}, bf16[512,512]{1,0:T(8,128)(2,1)}) custom-call(bf16[128,512]{1,0:T(8,128)(2,1)} %gate_ref.1, bf16[128,512]{1,0:T(8,128)(2,1)} %up_ref.1, bf16[512,512]{1,0:T(8,128)(2,1)} %w_hbm.1, s32[4,4]{1,0:T(4,128)} %mask_ref.3, bf16[128,256]{1,0:T(8,128)(2,1)} %cot_hbm.1), custom_call_target="tpu_custom_call" | custom-call | tf_op jit(solution)/shard_map/pallas_call | solution.py:448
  77.0 2.3 %shard_map.85 = (bf16[128,256]{1,0:T(8,128)(2,1)}, bf16[128,512]{1,0:T(8,128)(2,1)}, bf16[128,512]{1,0:T(8,128)(2,1)}, bf16[512,512]{1,0:T(8,128)(2,1)}) custom-call(bf16[128,512]{1,0:T(8,128)(2,1)} %gate_ref.1, bf16[128,512]{1,0:T(8,128)(2,1)} %up_ref.1, s32[4,4]{1,0:T(4,128)} %mask_ref.3, bf16[128,256]{1,0:T(8,128)(2,1)} %get-tuple-element.7.outr_ref, ...), custom_call_target="tpu_custom_call" | custom-call | tf_op jit(solution)/shard_map/pallas_call | solution.py:474

commit v5 on v4

--- a/solution.py
+++ b/solution.py
@@ -38,14 +38,14 @@
     return [(0, half - 1), (half - 1, nz - 3), (nz - 3, nz)]
 
 
-def kernel(nz, nq, gate_hbm, up_hbm, w_hbm, mask_ref, cot_hbm,
+def kernel(nz, nq, gate_hbm, up_hbm, w_hbm, mask_hbm, cot_hbm,
            out_hbm, dh_hbm, dw_hbm,
            gate_v, up_v, wm, cot_v, hall, call, cA, cB,
            yown, ysend, yprt, ysum, yrecv, osum, oB, out_v,
            rbuf, sbuf, pbuf, acc, accb,
            ld, ag_s, ag_r, rs_s, rs_r, cA_s, cA_r, cB_s, cB_r,
            cg_s, cg_r, rel_s, rel_r, yp_s, yp_r, yr_s, yr_r,
-           oB_s, oB_r, ov_s, ov_r, st, far_sem):
+           oB_s, oB_r, ov_s, ov_r, st, far_sem, mask_ref):
     z = lax.axis_index("row")
     col = lax.axis_index("col")
     p = lax.div(col, 2)
@@ -102,7 +102,7 @@
     loads = [local(a, b, ld.at[i]) for i, (a, b) in enumerate((
         (gate_hbm, gate_v), (up_hbm, up_v), (cot_hbm, cot_v),
         (w_hbm.at[pl.ds(mine, dw_h)], wm.at[pl.ds(0, dw_h)]),
-        (w_hbm.at[pl.ds(other, dw_h)], wm.at[pl.ds(dw_h, dw_h)])))]
+        (w_hbm.at[pl.ds(other, dw_h)], wm.at[pl.ds(dw_h, dw_h)]), (mask_hbm, mask_ref)))]
     for l in loads:
         l.start()
     loads[0].wait()
@@ -113,12 +113,16 @@
         l.wait()
     br, bc = mask_ref.shape
     bs = dr // br
-    for i in range(br):
-        row = lax.rem(c * (br // 2) + i, br)
-        for j in range(bc):
-            sl = (pl.ds(i * bs, bs), pl.ds(j * bs, bs))
-            keep = jnp.full((bs, bs), mask_ref[row, j], jnp.int32) > 0
-            wm[sl] = jnp.where(keep, wm[sl], jnp.zeros((bs, bs), BF16))
+
+    def keep_blocks(ref):
+        for i in range(br):
+            row = lax.rem(c * (br // 2) + i, br)
+            for j in range(bc):
+                sl = (pl.ds(i * bs, bs), pl.ds(j * bs, bs))
+                keep = jnp.full((bs, bs), mask_ref[row, j], jnp.int32) > 0
+                ref[sl] = jnp.where(keep, ref[sl], jnp.zeros((bs, bs), BF16))
+
+    keep_blocks(wm)
     pl.semaphore_wait(bar, len(near_z) + nq)
 
     def tell(n):
@@ -302,6 +306,7 @@
             acc[...] += v
         else:
             accb[...] = (acc[...] + v).astype(BF16)
+            keep_blocks(accb)
             local(accb.at[pl.ds(0, dw_h)], dw_hbm.at[pl.ds(mine, dw_h)], st.at[0]).start()
             local(accb.at[pl.ds(dw_h, dw_h)], dw_hbm.at[pl.ds(other, dw_h)], st.at[1]).start()
 
@@ -415,23 +420,28 @@
     local(out_v, out_hbm, st.at[3]).wait()
 
 
-def finish(gate_ref, up_ref, mask_ref, outr_ref, dh_ref, dw_ref, out_ref, dgate_ref, dup_ref, ddown_ref):
-    tok = gate_ref.shape[0]
-    for r in range(0, tok, 32):
-        rows = pl.ds(r, 32)
-        dh = dh_ref[rows, :]
-        g = gate_ref[rows, :].astype(F32)
+def finish(gate_any, up_any, outr_any, dh_any, dw_any, out_any, dgate_any, dup_any, ddown_any,
+           gate_v, up_v, dh_v, dgate_v, dup_v, sem):
+    def copy(a, b, i):
+        c = pltpu.make_async_copy(a, b, sem.at[i])
+        c.start()
+        return c
+
+    loads = [copy(a, b, i) for i, (a, b) in enumerate(((gate_any, gate_v), (up_any, up_v), (dh_any, dh_v)))]
+    stores = [copy(dw_any, ddown_any, 3), copy(outr_any, out_any, 4)]
+    for l in loads:
+        l.wait()
+    tok = gate_v.shape[0]
+    for r in range(0, tok, tok // 2):
+        rows = pl.ds(r, tok // 2)
+        dh = dh_v[rows, :]
+        g = gate_v[rows, :].astype(F32)
         sig = 1.0 / (1.0 + jnp.exp(-g))
-        dgate_ref[rows, :] = (dh * up_ref[rows, :].astype(F32) * sig * (1.0 + g * (1.0 - sig))).astype(BF16)
-        dup_ref[rows, :] = (dh * (g * sig)).astype(BF16)
-    br, bc = mask_ref.shape
-    bs = dw_ref.shape[0] // br
-    for i in range(br):
-        for j in range(bc):
-            sl = (pl.ds(i * bs, bs), pl.ds(j * bs, bs))
-            keep = jnp.full((bs, bs), mask_ref[i, j], jnp.int32) > 0
-            ddown_ref[sl] = jnp.where(keep, dw_ref[sl], jnp.zeros((bs, bs), BF16))
-    out_ref[...] = outr_ref[...]
+        dgate_v[rows, :] = (dh * up_v[rows, :].astype(F32) * sig * (1.0 + g * (1.0 - sig))).astype(BF16)
+        dup_v[rows, :] = (dh * (g * sig)).astype(BF16)
+    stores += [copy(dgate_v, dgate_any, 5), copy(dup_v, dup_any, 6)]
+    for l in stores:
+        l.wait()
 
 
 def body(nz, nq, gate_pre, up_pre, down_weight, block_mask, cotangent):
@@ -443,8 +453,8 @@
     dma = pltpu.SemaphoreType.DMA
     vm = pltpu.VMEM
     any_ = pl.BlockSpec(memory_space=pl.ANY)
-    vmem = pl.BlockSpec(memory_space=pltpu.VMEM)
-    smem = pl.BlockSpec(memory_space=pltpu.SMEM)
+    hbm = pl.BlockSpec(memory_space=pltpu.HBM)
+    pin = functools.partial(pltpu.with_memory_space_constraint, memory_space=pltpu.HBM)
     outr, dh, dwr = pl.pallas_call(
         functools.partial(kernel, nz, nq),
         out_shape=(
@@ -452,7 +462,7 @@
             jax.ShapeDtypeStruct((tok, ffc), F32),
             jax.ShapeDtypeStruct((dr, ffc), BF16),
         ),
-        in_specs=[any_, any_, any_, smem, any_],
+        in_specs=[hbm] * 5,
         out_specs=(any_,) * 3,
         scratch_shapes=[
             vm((tok, ffc), BF16), vm((tok, ffc), BF16), vm((dr, ffc), BF16), vm((tok, dw_h), BF16),
@@ -463,14 +473,14 @@
             vm((nz, TR, TC), BF16), vm((nz, TR, TC), BF16), vm((tok, dw_h), BF16),
             vm((2, half, tok, ffc), BF16), vm((2, half, tok, ffc), BF16),
             vm((2, 2, tok, ffc), F32), vm((dr, ffc), F32), vm((dr, ffc), BF16),
-            dma((5,)), dma, dma((2, SUB, half)), dma, dma((2, SUB, half)),
+            dma((6,)), dma, dma((2, SUB, half)), dma, dma((2, SUB, half)),
             dma, dma, dma, dma((3,)),
             dma, dma((3,)), dma, dma((3,)), dma, dma((nz,)), dma, dma((ng,)),
-            dma, dma, dma, dma, dma((4,)), pltpu.SemaphoreType.REGULAR((2,)),
+            dma, dma, dma, dma, dma((4,)), pltpu.SemaphoreType.REGULAR((2,)), pltpu.SMEM(block_mask.shape, jnp.int32),
         ],
         compiler_params=pltpu.CompilerParams(
-            collective_id=0, has_side_effects=True, vmem_limit_bytes=60 * 1024 * 1024),
-    )(gate_pre, up_pre, down_weight, block_mask, cotangent)
+            collective_id=0, has_side_effects=True, vmem_limit_bytes=24 * 1024 * 1024),
+    )(pin(gate_pre), pin(up_pre), pin(down_weight), pin(block_mask), pin(cotangent))
     return pl.pallas_call(
         finish,
         out_shape=(
@@ -479,9 +489,14 @@
             jax.ShapeDtypeStruct((tok, ffc), BF16),
             jax.ShapeDtypeStruct((dr, ffc), BF16),
         ),
-        in_specs=[vmem, vmem, smem, vmem, vmem, vmem],
-        out_specs=(vmem,) * 4,
-    )(gate_pre, up_pre, block_mask, outr, dh, dwr)
+        in_specs=[any_] * 5,
+        out_specs=(any_,) * 4,
+        scratch_shapes=[
+            vm((tok, ffc), BF16), vm((tok, ffc), BF16), vm((tok, ffc), F32), vm((tok, ffc), BF16), vm((tok, ffc), BF16),
+            dma((7,)),
+        ],
+        compiler_params=pltpu.CompilerParams(vmem_limit_bytes=8 * 1024 * 1024),
+    )(gate_pre, up_pre, outr, dh, dwr)
 
 
 def solution(mesh):

time: 80 us -> 78 us (0.975)
  Pallas kernels: 78.7 us -> 76.5 us
    pallas_call x1, Pallas kernels: 76.3 us -> 75.2 us  [body(): pl.pallas_call(functools.partial(kernel, nz, nq), out_shape=(jax.ShapeDty...]
    pallas_call x1, Pallas kernels: 2.34 us -> 1.31 us  [body(): pl.pallas_call(finish, out_shape=(jax.ShapeDtypeStruct((tok, dw_h), BF16)...]
where the time goes in v5:
time: 78 us; the launch traced here: 77.2 us
  Pallas kernels  76.5 us (98%)
    pallas_call x1, Pallas kernels, body(): pl.pallas_call(functools.partial(kernel, nz, nq), out_shape=(jax.ShapeDty...  75.2 us

profile of v5, /device:TPU:6, one launch (start us, length us, event | category | flops | bytes accessed | tf_op | source)
XLA Modules:
  0.0 77.2 jit_solution(1693726527366814737)
XLA Ops:
  0.6 0.0 copy-start.1
  0.6 0.0 copy-start
  0.7 75.2 %shard_map.84 = (bf16[128,256]{1,0:T(8,128)(2,1)S(1)}, f32[128,512]{1,0:T(8,128)S(1)}, bf16[512,512]{1,0:T(8,128)(2,1)S(1)}) custom-call(bf16[128,512]{1,0:T(8,128)(2,1)} %gate_any.1, bf16[128,512]{1,0:T(8,128)(2,1)} %up_any.1, bf16[512,512]{1,0:T(8,128)(2,1)} %w_hbm.1, s32[4,4]{1,0:T(4,128)} %mask_hbm.1, bf16[128,256]{1,0:T(8,128)(2,1)} %cot_hbm.1), custom_call_target="tpu_custom_call" | custom-call | tf_op jit(solution)/shard_map/pallas_call | solution.py:458
  75.8 0.0 copy-done.1
  75.8 0.0 copy-done
  75.8 1.3 %shard_map.85 = (bf16[128,256]{1,0:T(8,128)(2,1)}, bf16[128,512]{1,0:T(8,128)(2,1)}, bf16[128,512]{1,0:T(8,128)(2,1)}, bf16[512,512]{1,0:T(8,128)(2,1)}) custom-call(bf16[128,512]{1,0:T(8,128)(2,1)S(1)} %copy-done, bf16[128,512]{1,0:T(8,128)(2,1)S(1)} %copy-done.1, bf16[128,256]{1,0:T(8,128)(2,1)S(1)} %get-tuple-element.7.outr_any, ...), custom_call_target="tpu_custom_call" | custom-call | tf_op jit(solution)/shard_map/pallas_call | solution.py:484
Async XLA Ops:
  0.6 75.2 %copy-start.1 = (bf16[128,512]{1,0:T(8,128)(2,1)S(1)}, bf16[128,512]{1,0:T(8,128)(2,1)}, u32[]{:S(2)}) copy-start(bf16[128,512]{1,0:T(8,128)(2,1)} %up_any.1) | copy-start | bytes 393220
  0.6 75.2 %copy-start = (bf16[128,512]{1,0:T(8,128)(2,1)S(1)}, bf16[128,512]{1,0:T(8,128)(2,1)}, u32[]{:S(2)}) copy-start(bf16[128,512]{1,0:T(8,128)(2,1)} %gate_any.1) | copy-start | bytes 393220

commit v6 on v5

--- a/solution.py
+++ b/solution.py
@@ -45,7 +45,7 @@
            rbuf, sbuf, pbuf, acc, accb,
            ld, ag_s, ag_r, rs_s, rs_r, cA_s, cA_r, cB_s, cB_r,
            cg_s, cg_r, rel_s, rel_r, yp_s, yp_r, yr_s, yr_r,
-           oB_s, oB_r, ov_s, ov_r, st, far_sem, mask_ref):
+           oB_s, oB_r, ov_s, ov_r, st, far_sem, mask_ref, plane_sem):
     z = lax.axis_index("row")
     col = lax.axis_index("col")
     p = lax.div(col, 2)
@@ -93,9 +93,11 @@
     for k in near_z:
         pl.semaphore_signal(bar, inc=1, device_id=zdev(k), device_id_type=MESH)
 
-    @pl.loop(1, nq)
-    def _(k):
-        pl.semaphore_signal(bar, inc=1, device_id=qdev(qmod(p + k)), device_id_type=MESH)
+    side = 4 if big else 2
+    px, py = lax.div(p, side), lax.rem(p, side)
+    for k in range(1, side):
+        for q in (lax.rem(px + k, side) * side + py, px * side + lax.rem(py + k, side)):
+            pl.semaphore_signal(bar, inc=1, device_id=qdev(q), device_id_type=MESH)
 
     pl.semaphore_signal(bar, inc=1, device_id=pdev, device_id_type=MESH)
 
@@ -123,7 +125,9 @@
                 ref[sl] = jnp.where(keep, ref[sl], jnp.zeros((bs, bs), BF16))
 
     keep_blocks(wm)
-    pl.semaphore_wait(bar, len(near_z) + nq)
+    pl.semaphore_wait(bar, len(near_z) + 2 * (side - 1) + 1)
+    for k in range(1, side):
+        pl.semaphore_signal(plane_sem, inc=1, device_id=qdev(px * side + lax.rem(py + k, side)), device_id_type=MESH)
 
     def tell(n):
         for k in (2 << n, -(2 << n)):
@@ -232,11 +236,12 @@
     def ag_far(d, u, sg, src):
         remote(hall.at[src, sub(u)], hall.at[nz - 1, sub(u)], ag_s, ag_r.at[d, u, half - 1], zdev(2 * sg)).start()
 
-    cot_one()
     for d, u, sg, n in pairs:
         ag(d, u, sg, 0, src=0).start()
         if half == 2 and n == half:
             ag_far(d, u, sg, 0)
+    pl.semaphore_wait(plane_sem, side - 1)
+    cot_one()
     if big:
         hear(0)
         tell(1)
@@ -477,6 +482,7 @@
             dma, dma, dma, dma((3,)),
             dma, dma((3,)), dma, dma((3,)), dma, dma((nz,)), dma, dma((ng,)),
             dma, dma, dma, dma, dma((4,)), pltpu.SemaphoreType.REGULAR((2,)), pltpu.SMEM(block_mask.shape, jnp.int32),
+            pltpu.SemaphoreType.REGULAR,
         ],
         compiler_params=pltpu.CompilerParams(
             collective_id=0, has_side_effects=True, vmem_limit_bytes=24 * 1024 * 1024),

time: 78 us -> 77.5 us (level)
  the two profiles are of different devices: /device:TPU:6 before, /device:TPU:2 now
where the time goes in v6:
time: 77.5 us; the launch traced here: 77.4 us
  Pallas kernels  76.7 us (99%)
    pallas_call x1, Pallas kernels, body(): pl.pallas_call(functools.partial(kernel, nz, nq), out_shape=(jax.ShapeDty...  75.4 us

profile of v6, /device:TPU:2, one launch (start us, length us, event | category | flops | bytes accessed | tf_op | source)
XLA Modules:
  0.0 77.4 jit_solution(13770025432330041322)
XLA Ops:
  0.6 0.0 copy-start.1
  0.6 0.0 copy-start
  0.7 75.4 %shard_map.84 = (bf16[128,256]{1,0:T(8,128)(2,1)S(1)}, f32[128,512]{1,0:T(8,128)S(1)}, bf16[512,512]{1,0:T(8,128)(2,1)S(1)}) custom-call(bf16[128,512]{1,0:T(8,128)(2,1)} %gate_any.1, bf16[128,512]{1,0:T(8,128)(2,1)} %up_any.1, bf16[512,512]{1,0:T(8,128)(2,1)} %w_hbm.1, s32[4,4]{1,0:T(4,128)} %mask_hbm.1, bf16[128,256]{1,0:T(8,128)(2,1)} %cot_hbm.1), custom_call_target="tpu_custom_call" | custom-call | tf_op jit(solution)/shard_map/pallas_call | solution.py:463
  76.0 0.0 copy-done.1
  76.1 0.0 copy-done
  76.1 1.3 %shard_map.85 = (bf16[128,256]{1,0:T(8,128)(2,1)}, bf16[128,512]{1,0:T(8,128)(2,1)}, bf16[128,512]{1,0:T(8,128)(2,1)}, bf16[512,512]{1,0:T(8,128)(2,1)}) custom-call(bf16[128,512]{1,0:T(8,128)(2,1)S(1)} %copy-done, bf16[128,512]{1,0:T(8,128)(2,1)S(1)} %copy-done.1, bf16[128,256]{1,0:T(8,128)(2,1)S(1)} %get-tuple-element.7.outr_any, ...), custom_call_target="tpu_custom_call" | custom-call | tf_op jit(solution)/shard_map/pallas_call | solution.py:490
Async XLA Ops:
  0.6 75.4 %copy-start.1 = (bf16[128,512]{1,0:T(8,128)(2,1)S(1)}, bf16[128,512]{1,0:T(8,128)(2,1)}, u32[]{:S(2)}) copy-start(bf16[128,512]{1,0:T(8,128)(2,1)} %up_any.1) | copy-start | bytes 393220
  0.6 75.4 %copy-start = (bf16[128,512]{1,0:T(8,128)(2,1)S(1)}, bf16[128,512]{1,0:T(8,128)(2,1)}, u32[]{:S(2)}) copy-start(bf16[128,512]{1,0:T(8,128)(2,1)} %gate_any.1) | copy-start | bytes 393220
